TPU v7x, 256 devices: a whole 4x4x8 slice. The times are simulated.
256 devices in a mesh: mp: 8 (over x, core), ctx: 32 (over z, y).
Axes of the slice: x: 4, y: 4, z: 8, core: 2. Of those that a mesh axis runs over, the one named last changes fastest.
Arguments:
- queries: bfloat16 [262144, 1024], P(('mp', 'ctx')), parts along dimension 0, may hold values from -6 to 6
- key_rows: bfloat16 [262144, 1024], P(('mp', 'ctx')), parts along dimension 0, may hold values from -6 to 6
- value_rows: bfloat16 [262144, 1024], P(('mp', 'ctx')), parts along dimension 0, may hold values from -6 to 6
- conv_weight: float32 [24, 4, 1024], P('mp'), parts along dimension 0, may hold values from -3 to 3
- head_gain: float32 [8192], P('mp'), parts along dimension 0, may hold values from 0.1 to 1.9
Outputs:
- attended: bfloat16 [262144, 1024], P(('mp', 'ctx')), parts along dimension 0
There are 8 independent parts, one for each index of `mp`. A program takes and returns all parts, laid end to end along the dimension named above; each array names one. Nothing has to cross between parts.
All inputs are finite; a program needn't handle non-finite values.
Results may differ from a plain program's by a relative error of at most 0.006.
Values may be sent and summed in bfloat16 or wider, within the bound.
A program may use at most 128 MiB of HBM per device.

v0:
```python
import jax
import jax.numpy as jnp
from jax import lax
from jax.sharding import PartitionSpec as P

HDIM = 128
CONV = 4


def passed_along(value, axis, steps):
    count = lax.axis_size(axis)
    initial, last = (max(0, -steps), min(count, count - steps))
    return lax.ppermute(value, axis, [(source, source + steps) for source in range(initial, last)])


def causal_conv(rows, earlier, taps):
    tokens_here = rows.shape[0]
    padded = jnp.concatenate([earlier.astype(jnp.float32), rows.astype(jnp.float32)], axis=0)
    total = jnp.zeros((tokens_here, rows.shape[1]), jnp.float32)
    for tap in range(CONV):
        total = total + taps[tap][None, :] * padded[tap : tap + tokens_here]
    return total


def body(queries, key_rows, value_rows, conv_weight, head_gain):
    tokens_here = queries.shape[0]
    heads_n = head_gain.shape[0] // HDIM
    tails = jnp.stack(
        [
            queries[tokens_here - CONV + 1 :],
            key_rows[tokens_here - CONV + 1 :],
            value_rows[tokens_here - CONV + 1 :],
        ]
    )
    earlier = passed_along(tails, "ctx", 1)
    query_f = (
        jax.nn.silu(causal_conv(queries, earlier[0], conv_weight[0])) * HDIM ** (-0.5)
    ).astype(jnp.bfloat16)
    key_f = jax.nn.silu(causal_conv(key_rows, earlier[1], conv_weight[1])).astype(jnp.bfloat16)
    value_f = causal_conv(value_rows, earlier[2], conv_weight[2]).astype(jnp.bfloat16)
    query_h = query_f.reshape(tokens_here, heads_n, HDIM)
    key_h = key_f.reshape(tokens_here, heads_n, HDIM)
    value_h = value_f.reshape(tokens_here, heads_n, HDIM)
    local = jnp.einsum("shd,she->hde", key_h, value_h, preferred_element_type=jnp.float32)
    zeros_state = jnp.zeros_like(local)

    def relay_turn(turn_index, carry):
        incoming = passed_along(carry[1], "ctx", 1)
        return (incoming, incoming + local)

    prefix_sum, passed_on = lax.fori_loop(
        0, lax.axis_size("ctx") - 1, relay_turn, (zeros_state, local)
    )
    causal = jnp.arange(tokens_here)[:, None] >= jnp.arange(tokens_here)[None, :]
    scores = jnp.einsum("thd,shd->hts", query_h, key_h, preferred_element_type=jnp.float32)
    scores = jnp.where(causal[None], scores, 0.0).astype(jnp.bfloat16)
    inner = jnp.einsum("hts,she->the", scores, value_h, preferred_element_type=jnp.float32)
    cross = jnp.einsum(
        "thd,hde->the", query_h, prefix_sum.astype(jnp.bfloat16), preferred_element_type=jnp.float32
    )
    outputs = inner + cross
    scale_inv = lax.rsqrt(jnp.mean(outputs * outputs, axis=2, keepdims=True) + 1e-06)
    normed = outputs * scale_inv * head_gain.reshape(heads_n, HDIM)[None]
    return normed.reshape(tokens_here, heads_n * HDIM).astype(jnp.bfloat16)


def solution(mesh):
    return jax.shard_map(
        body,
        mesh=mesh,
        in_specs=(
            P(("mp", "ctx"), None),
            P(("mp", "ctx"), None),
            P(("mp", "ctx"), None),
            P("mp", None, None),
            P("mp"),
        ),
        out_specs=P(("mp", "ctx"), None),
        check_vma=False,
    )
```

profile of v0, /device:TPU:128, one launch (start us, length us, event | category | flops | bytes accessed | tf_op | source)
XLA Modules:
  0.0 609.5 jit_solution(10577825009094651985)
XLA Ops:
  1.7 3.5 collective-permute-start.1
  7.5 4.0 convert_element_type.58
  11.5 2.4 convert_element_type.54
  14.0 2.4 convert_element_type.50
  16.4 7.5 %multiply_convert_fusion = bf16[1024,1024]{1,0:T(8,128)(2,1)S(1)} fusion(f32[1024,1024]{1,0:T(8,128)} %convert_element_type.58, f32[3,1024]{1,0:T(4,128)S(1)} %get-tuple-element.48, f32[1024]{0:T(1024)S(1)} %bitcast.77, f32[1024]{0:T(1024)S(1)} %bitcast.78, f32[1024]{0:T(1024)S(1)} %bitcast.75, f32[1024]{0:T(1024)S(1)} %bitcast.76), kind=kLoop, calls=%fused_computation.44 | loop fusion | flops 15728640 | bytes 6320128 | tf_op jit(solution)/shard_map/convert_element_type | solution.py:39
  23.9 2.6 copy.13
  26.5 7.5 %fusion.39 = bf16[128,8,8,128]{3,2,1,0:T(8,128)(2,1)S(1)} fusion(f32[1024,1024]{1,0:T(8,128)} %convert_element_type.50, f32[1024]{0:T(1024)S(1)} %bitcast.72, f32[3,1024]{1,0:T(4,128)S(1)} %get-tuple-element.47, f32[1024]{0:T(1024)S(1)} %bitcast.73, f32[1024]{0:T(1024)S(1)} %bitcast.74, f32[1024]{0:T(1024)S(1)} %bitcast.71), kind=kLoop, calls=%fused_computation.53 | loop fusion | flops 11534336 | bytes 6320128
  37.2 2.8 fusion.40
  40.0 13.4 %fusion = f32[8,128,1024]{2,1,0:T(8,128)} fusion(pred[1024,1024]{1,0:T(8,128)(4,1)} %iota_compare_fusion, bf16[1024,8,128]{0,2,1:T(8,128)(2,1)} %bitcast.65, bf16[128,8,8,128]{3,2,1,0:T(8,128)(2,1)S(1)} %fusion.40, bf16[128,8,8,128]{3,2,1,0:T(8,128)(2,1)} %copy-done.4), kind=kOutput, calls=%fused_computation.1 | convolution fusion | flops 4311744512 | bytes 11534336 | tf_op jit(solution)/shard_map/hts,she->the/dot_general | solution.py:57
  53.4 549.7 %while.12 = (s32[]{:T(128)}, f32[8,128,128]{2,1,0:T(8,128)}, f32[8,128,128]{2,1,0:T(8,128)}, f32[8,128,128]{2,1,0:T(8,128)S(1)}, s32[]{:T(128)}) while((s32[]{:T(128)}, f32[8,128,128]{2,1,0:T(8,128)}, f32[8,128,128]{2,1,0:T(8,128)}, f32[8,128,128]{2,1,0:T(8,128)S(1)}, s32[]{:T(128)}) %tuple.33), condition=%wide.region_1.2_spmd, body=%wide.region_0.1_spmd.sunk | while | flops 131074 | bytes 5767297 | solution.py:51
  53.4 3.5 collective-permute-start
  56.9 15.3 %collective-permute-done = f32[8,128,128]{2,1,0:T(8,128)S(1)} collective-permute-done((f32[8,128,128]{2,1,0:T(8,128)}, f32[8,128,128]{2,1,0:T(8,128)S(1)}, u32[]{:S(2)}, u32[]{:S(2)}) %collective-permute-start) | collective-permute-done | bytes 524320 | tf_op jit(solution)/shard_map/while/body/eval_jaxpr/ppermute | solution.py:13
  73.2 1.9 collective-permute-start
  75.1 16.0 %collective-permute-done = f32[8,128,128]{2,1,0:T(8,128)S(1)} collective-permute-done((f32[8,128,128]{2,1,0:T(8,128)}, f32[8,128,128]{2,1,0:T(8,128)S(1)}, u32[]{:S(2)}, u32[]{:S(2)}) %collective-permute-start) | collective-permute-done | bytes 524320 | tf_op jit(solution)/shard_map/while/body/eval_jaxpr/ppermute | solution.py:13
  92.1 1.9 collective-permute-start
  94.0 15.0 %collective-permute-done = f32[8,128,128]{2,1,0:T(8,128)S(1)} collective-permute-done((f32[8,128,128]{2,1,0:T(8,128)}, f32[8,128,128]{2,1,0:T(8,128)S(1)}, u32[]{:S(2)}, u32[]{:S(2)}) %collective-permute-start) | collective-permute-done | bytes 524320 | tf_op jit(solution)/shard_map/while/body/eval_jaxpr/ppermute | solution.py:13
  110.1 1.9 collective-permute-start
  112.0 14.1 %collective-permute-done = f32[8,128,128]{2,1,0:T(8,128)S(1)} collective-permute-done((f32[8,128,128]{2,1,0:T(8,128)}, f32[8,128,128]{2,1,0:T(8,128)S(1)}, u32[]{:S(2)}, u32[]{:S(2)}) %collective-permute-start) | collective-permute-done | bytes 524320 | tf_op jit(solution)/shard_map/while/body/eval_jaxpr/ppermute | solution.py:13
  127.1 1.9 collective-permute-start
  129.1 13.2 %collective-permute-done = f32[8,128,128]{2,1,0:T(8,128)S(1)} collective-permute-done((f32[8,128,128]{2,1,0:T(8,128)}, f32[8,128,128]{2,1,0:T(8,128)S(1)}, u32[]{:S(2)}, u32[]{:S(2)}) %collective-permute-start) | collective-permute-done | bytes 524320 | tf_op jit(solution)/shard_map/while/body/eval_jaxpr/ppermute | solution.py:13
  145.2 12.7 %collective-permute-done = f32[8,128,128]{2,1,0:T(8,128)S(1)} collective-permute-done((f32[8,128,128]{2,1,0:T(8,128)}, f32[8,128,128]{2,1,0:T(8,128)S(1)}, u32[]{:S(2)}, u32[]{:S(2)}) %collective-permute-start) | collective-permute-done | bytes 524320 | tf_op jit(solution)/shard_map/while/body/eval_jaxpr/ppermute | solution.py:13
  160.8 12.7 %collective-permute-done = f32[8,128,128]{2,1,0:T(8,128)S(1)} collective-permute-done((f32[8,128,128]{2,1,0:T(8,128)}, f32[8,128,128]{2,1,0:T(8,128)S(1)}, u32[]{:S(2)}, u32[]{:S(2)}) %collective-permute-start) | collective-permute-done | bytes 524320 | tf_op jit(solution)/shard_map/while/body/eval_jaxpr/ppermute | solution.py:13
  176.4 12.7 %collective-permute-done = f32[8,128,128]{2,1,0:T(8,128)S(1)} collective-permute-done((f32[8,128,128]{2,1,0:T(8,128)}, f32[8,128,128]{2,1,0:T(8,128)S(1)}, u32[]{:S(2)}, u32[]{:S(2)}) %collective-permute-start) | collective-permute-done | bytes 524320 | tf_op jit(solution)/shard_map/while/body/eval_jaxpr/ppermute | solution.py:13
  192.0 13.2 %collective-permute-done = f32[8,128,128]{2,1,0:T(8,128)S(1)} collective-permute-done((f32[8,128,128]{2,1,0:T(8,128)}, f32[8,128,128]{2,1,0:T(8,128)S(1)}, u32[]{:S(2)}, u32[]{:S(2)}) %collective-permute-start) | collective-permute-done | bytes 524320 | tf_op jit(solution)/shard_map/while/body/eval_jaxpr/ppermute | solution.py:13
  208.2 14.3 %collective-permute-done = f32[8,128,128]{2,1,0:T(8,128)S(1)} collective-permute-done((f32[8,128,128]{2,1,0:T(8,128)}, f32[8,128,128]{2,1,0:T(8,128)S(1)}, u32[]{:S(2)}, u32[]{:S(2)}) %collective-permute-start) | collective-permute-done | bytes 524320 | tf_op jit(solution)/shard_map/while/body/eval_jaxpr/ppermute | solution.py:13
  225.4 15.4 %collective-permute-done = f32[8,128,128]{2,1,0:T(8,128)S(1)} collective-permute-done((f32[8,128,128]{2,1,0:T(8,128)}, f32[8,128,128]{2,1,0:T(8,128)S(1)}, u32[]{:S(2)}, u32[]{:S(2)}) %collective-permute-start) | collective-permute-done | bytes 524320 | tf_op jit(solution)/shard_map/while/body/eval_jaxpr/ppermute | solution.py:13
  243.7 16.5 %collective-permute-done = f32[8,128,128]{2,1,0:T(8,128)S(1)} collective-permute-done((f32[8,128,128]{2,1,0:T(8,128)}, f32[8,128,128]{2,1,0:T(8,128)S(1)}, u32[]{:S(2)}, u32[]{:S(2)}) %collective-permute-start) | collective-permute-done | bytes 524320 | tf_op jit(solution)/shard_map/while/body/eval_jaxpr/ppermute | solution.py:13
  263.1 17.7 %collective-permute-done = f32[8,128,128]{2,1,0:T(8,128)S(1)} collective-permute-done((f32[8,128,128]{2,1,0:T(8,128)}, f32[8,128,128]{2,1,0:T(8,128)S(1)}, u32[]{:S(2)}, u32[]{:S(2)}) %collective-permute-start) | collective-permute-done | bytes 524320 | tf_op jit(solution)/shard_map/while/body/eval_jaxpr/ppermute | solution.py:13
  283.7 17.8 %collective-permute-done = f32[8,128,128]{2,1,0:T(8,128)S(1)} collective-permute-done((f32[8,128,128]{2,1,0:T(8,128)}, f32[8,128,128]{2,1,0:T(8,128)S(1)}, u32[]{:S(2)}, u32[]{:S(2)}) %collective-permute-start) | collective-permute-done | bytes 524320 | tf_op jit(solution)/shard_map/while/body/eval_jaxpr/ppermute | solution.py:13
  304.4 17.0 %collective-permute-done = f32[8,128,128]{2,1,0:T(8,128)S(1)} collective-permute-done((f32[8,128,128]{2,1,0:T(8,128)}, f32[8,128,128]{2,1,0:T(8,128)S(1)}, u32[]{:S(2)}, u32[]{:S(2)}) %collective-permute-start) | collective-permute-done | bytes 524320 | tf_op jit(solution)/shard_map/while/body/eval_jaxpr/ppermute | solution.py:13
  324.4 16.1 %collective-permute-done = f32[8,128,128]{2,1,0:T(8,128)S(1)} collective-permute-done((f32[8,128,128]{2,1,0:T(8,128)}, f32[8,128,128]{2,1,0:T(8,128)S(1)}, u32[]{:S(2)}, u32[]{:S(2)}) %collective-permute-start) | collective-permute-done | bytes 524320 | tf_op jit(solution)/shard_map/while/body/eval_jaxpr/ppermute | solution.py:13
  343.4 15.2 %collective-permute-done = f32[8,128,128]{2,1,0:T(8,128)S(1)} collective-permute-done((f32[8,128,128]{2,1,0:T(8,128)}, f32[8,128,128]{2,1,0:T(8,128)S(1)}, u32[]{:S(2)}, u32[]{:S(2)}) %collective-permute-start) | collective-permute-done | bytes 524320 | tf_op jit(solution)/shard_map/while/body/eval_jaxpr/ppermute | solution.py:13
  361.5 14.3 %collective-permute-done = f32[8,128,128]{2,1,0:T(8,128)S(1)} collective-permute-done((f32[8,128,128]{2,1,0:T(8,128)}, f32[8,128,128]{2,1,0:T(8,128)S(1)}, u32[]{:S(2)}, u32[]{:S(2)}) %collective-permute-start) | collective-permute-done | bytes 524320 | tf_op jit(solution)/shard_map/while/body/eval_jaxpr/ppermute | solution.py:13
  378.7 13.3 %collective-permute-done = f32[8,128,128]{2,1,0:T(8,128)S(1)} collective-permute-done((f32[8,128,128]{2,1,0:T(8,128)}, f32[8,128,128]{2,1,0:T(8,128)S(1)}, u32[]{:S(2)}, u32[]{:S(2)}) %collective-permute-start) | collective-permute-done | bytes 524320 | tf_op jit(solution)/shard_map/while/body/eval_jaxpr/ppermute | solution.py:13
  395.0 12.7 %collective-permute-done = f32[8,128,128]{2,1,0:T(8,128)S(1)} collective-permute-done((f32[8,128,128]{2,1,0:T(8,128)}, f32[8,128,128]{2,1,0:T(8,128)S(1)}, u32[]{:S(2)}, u32[]{:S(2)}) %collective-permute-start) | collective-permute-done | bytes 524320 | tf_op jit(solution)/shard_map/while/body/eval_jaxpr/ppermute | solution.py:13
  410.6 12.7 %collective-permute-done = f32[8,128,128]{2,1,0:T(8,128)S(1)} collective-permute-done((f32[8,128,128]{2,1,0:T(8,128)}, f32[8,128,128]{2,1,0:T(8,128)S(1)}, u32[]{:S(2)}, u32[]{:S(2)}) %collective-permute-start) | collective-permute-done | bytes 524320 | tf_op jit(solution)/shard_map/while/body/eval_jaxpr/ppermute | solution.py:13
  426.2 12.7 %collective-permute-done = f32[8,128,128]{2,1,0:T(8,128)S(1)} collective-permute-done((f32[8,128,128]{2,1,0:T(8,128)}, f32[8,128,128]{2,1,0:T(8,128)S(1)}, u32[]{:S(2)}, u32[]{:S(2)}) %collective-permute-start) | collective-permute-done | bytes 524320 | tf_op jit(solution)/shard_map/while/body/eval_jaxpr/ppermute | solution.py:13
  441.8 13.1 %collective-permute-done = f32[8,128,128]{2,1,0:T(8,128)S(1)} collective-permute-done((f32[8,128,128]{2,1,0:T(8,128)}, f32[8,128,128]{2,1,0:T(8,128)S(1)}, u32[]{:S(2)}, u32[]{:S(2)}) %collective-permute-start) | collective-permute-done | bytes 524320 | tf_op jit(solution)/shard_map/while/body/eval_jaxpr/ppermute | solution.py:13
  457.8 14.2 %collective-permute-done = f32[8,128,128]{2,1,0:T(8,128)S(1)} collective-permute-done((f32[8,128,128]{2,1,0:T(8,128)}, f32[8,128,128]{2,1,0:T(8,128)S(1)}, u32[]{:S(2)}, u32[]{:S(2)}) %collective-permute-start) | collective-permute-done | bytes 524320 | tf_op jit(solution)/shard_map/while/body/eval_jaxpr/ppermute | solution.py:13
  474.9 15.3 %collective-permute-done = f32[8,128,128]{2,1,0:T(8,128)S(1)} collective-permute-done((f32[8,128,128]{2,1,0:T(8,128)}, f32[8,128,128]{2,1,0:T(8,128)S(1)}, u32[]{:S(2)}, u32[]{:S(2)}) %collective-permute-start) | collective-permute-done | bytes 524320 | tf_op jit(solution)/shard_map/while/body/eval_jaxpr/ppermute | solution.py:13
  493.1 16.3 %collective-permute-done = f32[8,128,128]{2,1,0:T(8,128)S(1)} collective-permute-done((f32[8,128,128]{2,1,0:T(8,128)}, f32[8,128,128]{2,1,0:T(8,128)S(1)}, u32[]{:S(2)}, u32[]{:S(2)}) %collective-permute-start) | collective-permute-done | bytes 524320 | tf_op jit(solution)/shard_map/while/body/eval_jaxpr/ppermute | solution.py:13
  512.4 17.5 %collective-permute-done = f32[8,128,128]{2,1,0:T(8,128)S(1)} collective-permute-done((f32[8,128,128]{2,1,0:T(8,128)}, f32[8,128,128]{2,1,0:T(8,128)S(1)}, u32[]{:S(2)}, u32[]{:S(2)}) %collective-permute-start) | collective-permute-done | bytes 524320 | tf_op jit(solution)/shard_map/while/body/eval_jaxpr/ppermute | solution.py:13
  532.8 17.9 %collective-permute-done = f32[8,128,128]{2,1,0:T(8,128)S(1)} collective-permute-done((f32[8,128,128]{2,1,0:T(8,128)}, f32[8,128,128]{2,1,0:T(8,128)S(1)}, u32[]{:S(2)}, u32[]{:S(2)}) %collective-permute-start) | collective-permute-done | bytes 524320 | tf_op jit(solution)/shard_map/while/body/eval_jaxpr/ppermute | solution.py:13
  553.7 17.2 %collective-permute-done = f32[8,128,128]{2,1,0:T(8,128)S(1)} collective-permute-done((f32[8,128,128]{2,1,0:T(8,128)}, f32[8,128,128]{2,1,0:T(8,128)S(1)}, u32[]{:S(2)}, u32[]{:S(2)}) %collective-permute-start) | collective-permute-done | bytes 524320 | tf_op jit(solution)/shard_map/while/body/eval_jaxpr/ppermute | solution.py:13
  573.8 12.7 %collective-permute-done = f32[8,128,128]{2,1,0:T(8,128)S(1)} collective-permute-done((f32[8,128,128]{2,1,0:T(8,128)}, f32[8,128,128]{2,1,0:T(8,128)S(1)}, u32[]{:S(2)}, u32[]{:S(2)}) %collective-permute-start) | collective-permute-done | bytes 524320 | tf_op jit(solution)/shard_map/while/body/eval_jaxpr/ppermute | solution.py:13
  589.4 12.7 %collective-permute-done = f32[8,128,128]{2,1,0:T(8,128)S(1)} collective-permute-done((f32[8,128,128]{2,1,0:T(8,128)}, f32[8,128,128]{2,1,0:T(8,128)S(1)}, u32[]{:S(2)}, u32[]{:S(2)}) %collective-permute-start) | collective-permute-done | bytes 524320 | tf_op jit(solution)/shard_map/while/body/eval_jaxpr/ppermute | solution.py:13
  603.1 3.3 fusion.30
  606.9 2.6 copy.9
  (143 shorter events, 88.7 us)
Async XLA Ops:
  0.0 11.5 %copy-start.2 = (bf16[1024,1024]{1,0:T(8,128)(2,1)S(1)}, bf16[1024,1024]{1,0:T(8,128)(2,1)}, u32[]{:S(2)}) copy-start(bf16[1024,1024]{1,0:T(8,128)(2,1)} %param.7) | copy-start | bytes 6291460
  1.7 14.7 %collective-permute-start.1 = (bf16[3,3,1024]{2,1,0:T(4,128)(2,1)S(1)}, bf16[3,3,1024]{2,1,0:T(4,128)(2,1)S(1)}, u32[]{:S(2)}, u32[]{:S(2)}) collective-permute-start(bf16[3,3,1024]{2,1,0:T(4,128)(2,1)S(1)} %pad_maximum_fusion.3), channel_id=1, source_target_pairs={{0,1},{1,2},{2,3},{3,4},{4,5},{5,6},{6,7},{7,8},{8,9},{9,10},{10,1... | collective-permute-start | bytes 55304 | tf_op jit(solution)/shard_map/ppermute | solution.py:13
  11.5 2.4 copy-start.3
  26.5 7.5 %copy-start.5 = (bf16[1024,1024]{0,1:T(8,128)(2,1)S(1)}, bf16[1024,1024]{0,1:T(8,128)(2,1)}, u32[]{:S(2)}) copy-start(bf16[1024,1024]{0,1:T(8,128)(2,1)} %copy.13) | copy-start | bytes 6291460
  34.0 1.6 copy-start.4
  34.0 3.1 copy-start.1
  53.4 18.8 %collective-permute-start = (f32[8,128,128]{2,1,0:T(8,128)}, f32[8,128,128]{2,1,0:T(8,128)S(1)}, u32[]{:S(2)}, u32[]{:S(2)}) collective-permute-start(f32[8,128,128]{2,1,0:T(8,128)} %get-tuple-element.84), channel_id=1, source_target_pairs={{0,1},{1,2},{2,3},{3,4},{4,5},{5,6},{6,7},{7,8},{8,9},{9,10},{10,1... | collective-permute-start | bytes 1572872 | tf_op jit(solution)/shard_map/while/body/eval_jaxpr/ppermute | solution.py:13
  72.2 1.0 copy-start
  73.2 17.9 %collective-permute-start = (f32[8,128,128]{2,1,0:T(8,128)}, f32[8,128,128]{2,1,0:T(8,128)S(1)}, u32[]{:S(2)}, u32[]{:S(2)}) collective-permute-start(f32[8,128,128]{2,1,0:T(8,128)} %get-tuple-element.84), channel_id=1, source_target_pairs={{0,1},{1,2},{2,3},{3,4},{4,5},{5,6},{6,7},{7,8},{8,9},{9,10},{10,1... | collective-permute-start | bytes 1572872 | tf_op jit(solution)/shard_map/while/body/eval_jaxpr/ppermute | solution.py:13
  91.1 1.0 copy-start
  92.1 17.0 %collective-permute-start = (f32[8,128,128]{2,1,0:T(8,128)}, f32[8,128,128]{2,1,0:T(8,128)S(1)}, u32[]{:S(2)}, u32[]{:S(2)}) collective-permute-start(f32[8,128,128]{2,1,0:T(8,128)} %get-tuple-element.84), channel_id=1, source_target_pairs={{0,1},{1,2},{2,3},{3,4},{4,5},{5,6},{6,7},{7,8},{8,9},{9,10},{10,1... | collective-permute-start | bytes 1572872 | tf_op jit(solution)/shard_map/while/body/eval_jaxpr/ppermute | solution.py:13
  109.1 1.0 copy-start
  110.1 16.0 %collective-permute-start = (f32[8,128,128]{2,1,0:T(8,128)}, f32[8,128,128]{2,1,0:T(8,128)S(1)}, u32[]{:S(2)}, u32[]{:S(2)}) collective-permute-start(f32[8,128,128]{2,1,0:T(8,128)} %get-tuple-element.84), channel_id=1, source_target_pairs={{0,1},{1,2},{2,3},{3,4},{4,5},{5,6},{6,7},{7,8},{8,9},{9,10},{10,1... | collective-permute-start | bytes 1572872 | tf_op jit(solution)/shard_map/while/body/eval_jaxpr/ppermute | solution.py:13
  126.1 1.0 copy-start
  127.1 15.1 %collective-permute-start = (f32[8,128,128]{2,1,0:T(8,128)}, f32[8,128,128]{2,1,0:T(8,128)S(1)}, u32[]{:S(2)}, u32[]{:S(2)}) collective-permute-start(f32[8,128,128]{2,1,0:T(8,128)} %get-tuple-element.84), channel_id=1, source_target_pairs={{0,1},{1,2},{2,3},{3,4},{4,5},{5,6},{6,7},{7,8},{8,9},{9,10},{10,1... | collective-permute-start | bytes 1572872 | tf_op jit(solution)/shard_map/while/body/eval_jaxpr/ppermute | solution.py:13
  142.3 1.0 copy-start
  143.3 14.6 %collective-permute-start = (f32[8,128,128]{2,1,0:T(8,128)}, f32[8,128,128]{2,1,0:T(8,128)S(1)}, u32[]{:S(2)}, u32[]{:S(2)}) collective-permute-start(f32[8,128,128]{2,1,0:T(8,128)} %get-tuple-element.84), channel_id=1, source_target_pairs={{0,1},{1,2},{2,3},{3,4},{4,5},{5,6},{6,7},{7,8},{8,9},{9,10},{10,1... | collective-permute-start | bytes 1572872 | tf_op jit(solution)/shard_map/while/body/eval_jaxpr/ppermute | solution.py:13
  157.9 1.0 copy-start
  158.9 14.6 %collective-permute-start = (f32[8,128,128]{2,1,0:T(8,128)}, f32[8,128,128]{2,1,0:T(8,128)S(1)}, u32[]{:S(2)}, u32[]{:S(2)}) collective-permute-start(f32[8,128,128]{2,1,0:T(8,128)} %get-tuple-element.84), channel_id=1, source_target_pairs={{0,1},{1,2},{2,3},{3,4},{4,5},{5,6},{6,7},{7,8},{8,9},{9,10},{10,1... | collective-permute-start | bytes 1572872 | tf_op jit(solution)/shard_map/while/body/eval_jaxpr/ppermute | solution.py:13
  173.5 1.0 copy-start
  174.5 14.6 %collective-permute-start = (f32[8,128,128]{2,1,0:T(8,128)}, f32[8,128,128]{2,1,0:T(8,128)S(1)}, u32[]{:S(2)}, u32[]{:S(2)}) collective-permute-start(f32[8,128,128]{2,1,0:T(8,128)} %get-tuple-element.84), channel_id=1, source_target_pairs={{0,1},{1,2},{2,3},{3,4},{4,5},{5,6},{6,7},{7,8},{8,9},{9,10},{10,1... | collective-permute-start | bytes 1572872 | tf_op jit(solution)/shard_map/while/body/eval_jaxpr/ppermute | solution.py:13
  190.1 15.1 %collective-permute-start = (f32[8,128,128]{2,1,0:T(8,128)}, f32[8,128,128]{2,1,0:T(8,128)S(1)}, u32[]{:S(2)}, u32[]{:S(2)}) collective-permute-start(f32[8,128,128]{2,1,0:T(8,128)} %get-tuple-element.84), channel_id=1, source_target_pairs={{0,1},{1,2},{2,3},{3,4},{4,5},{5,6},{6,7},{7,8},{8,9},{9,10},{10,1... | collective-permute-start | bytes 1572872 | tf_op jit(solution)/shard_map/while/body/eval_jaxpr/ppermute | solution.py:13
  206.3 16.2 %collective-permute-start = (f32[8,128,128]{2,1,0:T(8,128)}, f32[8,128,128]{2,1,0:T(8,128)S(1)}, u32[]{:S(2)}, u32[]{:S(2)}) collective-permute-start(f32[8,128,128]{2,1,0:T(8,128)} %get-tuple-element.84), channel_id=1, source_target_pairs={{0,1},{1,2},{2,3},{3,4},{4,5},{5,6},{6,7},{7,8},{8,9},{9,10},{10,1... | collective-permute-start | bytes 1572872 | tf_op jit(solution)/shard_map/while/body/eval_jaxpr/ppermute | solution.py:13
  223.5 17.3 %collective-permute-start = (f32[8,128,128]{2,1,0:T(8,128)}, f32[8,128,128]{2,1,0:T(8,128)S(1)}, u32[]{:S(2)}, u32[]{:S(2)}) collective-permute-start(f32[8,128,128]{2,1,0:T(8,128)} %get-tuple-element.84), channel_id=1, source_target_pairs={{0,1},{1,2},{2,3},{3,4},{4,5},{5,6},{6,7},{7,8},{8,9},{9,10},{10,1... | collective-permute-start | bytes 1572872 | tf_op jit(solution)/shard_map/while/body/eval_jaxpr/ppermute | solution.py:13
  241.8 18.4 %collective-permute-start = (f32[8,128,128]{2,1,0:T(8,128)}, f32[8,128,128]{2,1,0:T(8,128)S(1)}, u32[]{:S(2)}, u32[]{:S(2)}) collective-permute-start(f32[8,128,128]{2,1,0:T(8,128)} %get-tuple-element.84), channel_id=1, source_target_pairs={{0,1},{1,2},{2,3},{3,4},{4,5},{5,6},{6,7},{7,8},{8,9},{9,10},{10,1... | collective-permute-start | bytes 1572872 | tf_op jit(solution)/shard_map/while/body/eval_jaxpr/ppermute | solution.py:13
  261.2 19.6 %collective-permute-start = (f32[8,128,128]{2,1,0:T(8,128)}, f32[8,128,128]{2,1,0:T(8,128)S(1)}, u32[]{:S(2)}, u32[]{:S(2)}) collective-permute-start(f32[8,128,128]{2,1,0:T(8,128)} %get-tuple-element.84), channel_id=1, source_target_pairs={{0,1},{1,2},{2,3},{3,4},{4,5},{5,6},{6,7},{7,8},{8,9},{9,10},{10,1... | collective-permute-start | bytes 1572872 | tf_op jit(solution)/shard_map/while/body/eval_jaxpr/ppermute | solution.py:13
  281.8 19.7 %collective-permute-start = (f32[8,128,128]{2,1,0:T(8,128)}, f32[8,128,128]{2,1,0:T(8,128)S(1)}, u32[]{:S(2)}, u32[]{:S(2)}) collective-permute-start(f32[8,128,128]{2,1,0:T(8,128)} %get-tuple-element.84), channel_id=1, source_target_pairs={{0,1},{1,2},{2,3},{3,4},{4,5},{5,6},{6,7},{7,8},{8,9},{9,10},{10,1... | collective-permute-start | bytes 1572872 | tf_op jit(solution)/shard_map/while/body/eval_jaxpr/ppermute | solution.py:13
  302.5 18.9 %collective-permute-start = (f32[8,128,128]{2,1,0:T(8,128)}, f32[8,128,128]{2,1,0:T(8,128)S(1)}, u32[]{:S(2)}, u32[]{:S(2)}) collective-permute-start(f32[8,128,128]{2,1,0:T(8,128)} %get-tuple-element.84), channel_id=1, source_target_pairs={{0,1},{1,2},{2,3},{3,4},{4,5},{5,6},{6,7},{7,8},{8,9},{9,10},{10,1... | collective-permute-start | bytes 1572872 | tf_op jit(solution)/shard_map/while/body/eval_jaxpr/ppermute | solution.py:13
  321.4 1.0 copy-start
  322.5 18.0 %collective-permute-start = (f32[8,128,128]{2,1,0:T(8,128)}, f32[8,128,128]{2,1,0:T(8,128)S(1)}, u32[]{:S(2)}, u32[]{:S(2)}) collective-permute-start(f32[8,128,128]{2,1,0:T(8,128)} %get-tuple-element.84), channel_id=1, source_target_pairs={{0,1},{1,2},{2,3},{3,4},{4,5},{5,6},{6,7},{7,8},{8,9},{9,10},{10,1... | collective-permute-start | bytes 1572872 | tf_op jit(solution)/shard_map/while/body/eval_jaxpr/ppermute | solution.py:13
  341.5 17.1 %collective-permute-start = (f32[8,128,128]{2,1,0:T(8,128)}, f32[8,128,128]{2,1,0:T(8,128)S(1)}, u32[]{:S(2)}, u32[]{:S(2)}) collective-permute-start(f32[8,128,128]{2,1,0:T(8,128)} %get-tuple-element.84), channel_id=1, source_target_pairs={{0,1},{1,2},{2,3},{3,4},{4,5},{5,6},{6,7},{7,8},{8,9},{9,10},{10,1... | collective-permute-start | bytes 1572872 | tf_op jit(solution)/shard_map/while/body/eval_jaxpr/ppermute | solution.py:13
  359.6 16.2 %collective-permute-start = (f32[8,128,128]{2,1,0:T(8,128)}, f32[8,128,128]{2,1,0:T(8,128)S(1)}, u32[]{:S(2)}, u32[]{:S(2)}) collective-permute-start(f32[8,128,128]{2,1,0:T(8,128)} %get-tuple-element.84), channel_id=1, source_target_pairs={{0,1},{1,2},{2,3},{3,4},{4,5},{5,6},{6,7},{7,8},{8,9},{9,10},{10,1... | collective-permute-start | bytes 1572872 | tf_op jit(solution)/shard_map/while/body/eval_jaxpr/ppermute | solution.py:13
  376.8 15.2 %collective-permute-start = (f32[8,128,128]{2,1,0:T(8,128)}, f32[8,128,128]{2,1,0:T(8,128)S(1)}, u32[]{:S(2)}, u32[]{:S(2)}) collective-permute-start(f32[8,128,128]{2,1,0:T(8,128)} %get-tuple-element.84), channel_id=1, source_target_pairs={{0,1},{1,2},{2,3},{3,4},{4,5},{5,6},{6,7},{7,8},{8,9},{9,10},{10,1... | collective-permute-start | bytes 1572872 | tf_op jit(solution)/shard_map/while/body/eval_jaxpr/ppermute | solution.py:13
  393.0 14.6 %collective-permute-start = (f32[8,128,128]{2,1,0:T(8,128)}, f32[8,128,128]{2,1,0:T(8,128)S(1)}, u32[]{:S(2)}, u32[]{:S(2)}) collective-permute-start(f32[8,128,128]{2,1,0:T(8,128)} %get-tuple-element.84), channel_id=1, source_target_pairs={{0,1},{1,2},{2,3},{3,4},{4,5},{5,6},{6,7},{7,8},{8,9},{9,10},{10,1... | collective-permute-start | bytes 1572872 | tf_op jit(solution)/shard_map/while/body/eval_jaxpr/ppermute | solution.py:13
  408.6 14.6 %collective-permute-start = (f32[8,128,128]{2,1,0:T(8,128)}, f32[8,128,128]{2,1,0:T(8,128)S(1)}, u32[]{:S(2)}, u32[]{:S(2)}) collective-permute-start(f32[8,128,128]{2,1,0:T(8,128)} %get-tuple-element.84), channel_id=1, source_target_pairs={{0,1},{1,2},{2,3},{3,4},{4,5},{5,6},{6,7},{7,8},{8,9},{9,10},{10,1... | collective-permute-start | bytes 1572872 | tf_op jit(solution)/shard_map/while/body/eval_jaxpr/ppermute | solution.py:13
  423.2 1.0 copy-start
  424.3 14.6 %collective-permute-start = (f32[8,128,128]{2,1,0:T(8,128)}, f32[8,128,128]{2,1,0:T(8,128)S(1)}, u32[]{:S(2)}, u32[]{:S(2)}) collective-permute-start(f32[8,128,128]{2,1,0:T(8,128)} %get-tuple-element.84), channel_id=1, source_target_pairs={{0,1},{1,2},{2,3},{3,4},{4,5},{5,6},{6,7},{7,8},{8,9},{9,10},{10,1... | collective-permute-start | bytes 1572872 | tf_op jit(solution)/shard_map/while/body/eval_jaxpr/ppermute | solution.py:13
  439.9 15.0 %collective-permute-start = (f32[8,128,128]{2,1,0:T(8,128)}, f32[8,128,128]{2,1,0:T(8,128)S(1)}, u32[]{:S(2)}, u32[]{:S(2)}) collective-permute-start(f32[8,128,128]{2,1,0:T(8,128)} %get-tuple-element.84), channel_id=1, source_target_pairs={{0,1},{1,2},{2,3},{3,4},{4,5},{5,6},{6,7},{7,8},{8,9},{9,10},{10,1... | collective-permute-start | bytes 1572872 | tf_op jit(solution)/shard_map/while/body/eval_jaxpr/ppermute | solution.py:13
  455.9 16.1 %collective-permute-start = (f32[8,128,128]{2,1,0:T(8,128)}, f32[8,128,128]{2,1,0:T(8,128)S(1)}, u32[]{:S(2)}, u32[]{:S(2)}) collective-permute-start(f32[8,128,128]{2,1,0:T(8,128)} %get-tuple-element.84), channel_id=1, source_target_pairs={{0,1},{1,2},{2,3},{3,4},{4,5},{5,6},{6,7},{7,8},{8,9},{9,10},{10,1... | collective-permute-start | bytes 1572872 | tf_op jit(solution)/shard_map/while/body/eval_jaxpr/ppermute | solution.py:13
  473.0 17.2 %collective-permute-start = (f32[8,128,128]{2,1,0:T(8,128)}, f32[8,128,128]{2,1,0:T(8,128)S(1)}, u32[]{:S(2)}, u32[]{:S(2)}) collective-permute-start(f32[8,128,128]{2,1,0:T(8,128)} %get-tuple-element.84), channel_id=1, source_target_pairs={{0,1},{1,2},{2,3},{3,4},{4,5},{5,6},{6,7},{7,8},{8,9},{9,10},{10,1... | collective-permute-start | bytes 1572872 | tf_op jit(solution)/shard_map/while/body/eval_jaxpr/ppermute | solution.py:13
  491.2 18.3 %collective-permute-start = (f32[8,128,128]{2,1,0:T(8,128)}, f32[8,128,128]{2,1,0:T(8,128)S(1)}, u32[]{:S(2)}, u32[]{:S(2)}) collective-permute-start(f32[8,128,128]{2,1,0:T(8,128)} %get-tuple-element.84), channel_id=1, source_target_pairs={{0,1},{1,2},{2,3},{3,4},{4,5},{5,6},{6,7},{7,8},{8,9},{9,10},{10,1... | collective-permute-start | bytes 1572872 | tf_op jit(solution)/shard_map/while/body/eval_jaxpr/ppermute | solution.py:13
  510.5 19.4 %collective-permute-start = (f32[8,128,128]{2,1,0:T(8,128)}, f32[8,128,128]{2,1,0:T(8,128)S(1)}, u32[]{:S(2)}, u32[]{:S(2)}) collective-permute-start(f32[8,128,128]{2,1,0:T(8,128)} %get-tuple-element.84), channel_id=1, source_target_pairs={{0,1},{1,2},{2,3},{3,4},{4,5},{5,6},{6,7},{7,8},{8,9},{9,10},{10,1... | collective-permute-start | bytes 1572872 | tf_op jit(solution)/shard_map/while/body/eval_jaxpr/ppermute | solution.py:13
  530.9 19.8 %collective-permute-start = (f32[8,128,128]{2,1,0:T(8,128)}, f32[8,128,128]{2,1,0:T(8,128)S(1)}, u32[]{:S(2)}, u32[]{:S(2)}) collective-permute-start(f32[8,128,128]{2,1,0:T(8,128)} %get-tuple-element.84), channel_id=1, source_target_pairs={{0,1},{1,2},{2,3},{3,4},{4,5},{5,6},{6,7},{7,8},{8,9},{9,10},{10,1... | collective-permute-start | bytes 1572872 | tf_op jit(solution)/shard_map/while/body/eval_jaxpr/ppermute | solution.py:13
  551.8 19.1 %collective-permute-start = (f32[8,128,128]{2,1,0:T(8,128)}, f32[8,128,128]{2,1,0:T(8,128)S(1)}, u32[]{:S(2)}, u32[]{:S(2)}) collective-permute-start(f32[8,128,128]{2,1,0:T(8,128)} %get-tuple-element.84), channel_id=1, source_target_pairs={{0,1},{1,2},{2,3},{3,4},{4,5},{5,6},{6,7},{7,8},{8,9},{9,10},{10,1... | collective-permute-start | bytes 1572872 | tf_op jit(solution)/shard_map/while/body/eval_jaxpr/ppermute | solution.py:13
  571.9 14.6 %collective-permute-start = (f32[8,128,128]{2,1,0:T(8,128)}, f32[8,128,128]{2,1,0:T(8,128)S(1)}, u32[]{:S(2)}, u32[]{:S(2)}) collective-permute-start(f32[8,128,128]{2,1,0:T(8,128)} %get-tuple-element.84), channel_id=1, source_target_pairs={{0,1},{1,2},{2,3},{3,4},{4,5},{5,6},{6,7},{7,8},{8,9},{9,10},{10,1... | collective-permute-start | bytes 1572872 | tf_op jit(solution)/shard_map/while/body/eval_jaxpr/ppermute | solution.py:13
  587.5 14.6 %collective-permute-start = (f32[8,128,128]{2,1,0:T(8,128)}, f32[8,128,128]{2,1,0:T(8,128)S(1)}, u32[]{:S(2)}, u32[]{:S(2)}) collective-permute-start(f32[8,128,128]{2,1,0:T(8,128)} %get-tuple-element.84), channel_id=1, source_target_pairs={{0,1},{1,2},{2,3},{3,4},{4,5},{5,6},{6,7},{7,8},{8,9},{9,10},{10,1... | collective-permute-start | bytes 1572872 | tf_op jit(solution)/shard_map/while/body/eval_jaxpr/ppermute | solution.py:13
  602.1 1.0 copy-start
  603.1 3.4 copy-start.6
  (21 other events, 21.3 us)
where the time goes:
time: 611 us; the launch traced here: 609 us
  waiting for transfers between devices  457 us (75%)
  starting transfers between devices  64.2 us (11%)
  other arithmetic  57.8 us (9%)
  matrix products  17.5 us (3%)
  local copies, waits for them, and re-layouts  12.4 us (2%)
    ppermute x32, waiting for transfers between devices, passed_along(): lax.ppermute(value, axis, [(source, source + steps) for source in range(i...  457 us
    ppermute x32, starting transfers between devices, passed_along(): lax.ppermute(value, axis, [(source, source + steps) for source in range(i...  64.2 us
    add x31, other arithmetic, relay_turn(): return (incoming, incoming + local)  29.2 us
    dot_general x1, matrix products, body(): jnp.einsum('hts,she->the', scores, value_h, preferred_element_type=jnp.fl...  13.4 us
  transfers between devices with their start and end apart: 32, of which 31 were waited for; matrix products, arithmetic and copies ran while one was open for 2% of the time, Pallas kernels for 0%

commit v1 on v0

v1 whole, which is shorter than its diff:
```python
import functools

import jax
import jax.numpy as jnp
from jax import lax
from jax.experimental import pallas as pl
from jax.experimental.pallas import tpu as pltpu
from jax.sharding import PartitionSpec as P

HDIM = 128
CONV = 4
PAD = 16
CHUNK = 256
MESH = pl.DeviceIdType.MESH


def conv_half(rows_ref, weights, chunk, lanes):
    rows = rows_ref[pl.ds(pl.multiple_of(chunk * CHUNK, CHUNK), CHUNK + PAD), lanes].astype(jnp.float32)
    back1 = pltpu.roll(rows, 1, 0)
    late = weights[3] * rows + weights[2] * back1
    early = weights[1] * rows + weights[0] * back1
    return (late + pltpu.roll(early, 2, 0))[PAD:]


def kernel(
    n, heads, tokens,
    q_hbm, k_hbm, v_hbm, w_hbm, g_hbm, out_hbm,
    q_raw, k_raw, v_raw, w_ref, g_ref, q_feat, k_feat, v_feat,
    inner, states, send1, land1, send2, land2, out_buf,
    load_sems, halo_send, halo_recv, send1_sems, recv1_sems, send2_sems, recv2_sems, out_sems,
):
    me = lax.axis_index("ctx")
    chunks = tokens // CHUNK
    piece = heads * HDIM // n
    per_head = HDIM // piece
    raws, hbms = (q_raw, k_raw, v_raw), (q_hbm, k_hbm, v_hbm)

    barrier = pltpu.get_barrier_semaphore()
    for step in range(1, n):
        pl.semaphore_signal(barrier, inc=1, device_id={"ctx": lax.rem(me + step, n)}, device_id_type=MESH)

    small = [
        pltpu.make_async_copy(w_hbm, w_ref, load_sems.at[3 * chunks]),
        pltpu.make_async_copy(g_hbm, g_ref, load_sems.at[3 * chunks + 1]),
    ]
    loads = {}
    for kind in range(3):
        for chunk in range(chunks):
            loads[kind, chunk] = pltpu.make_async_copy(
                hbms[kind].at[pl.ds(chunk * CHUNK, CHUNK)],
                raws[kind].at[pl.ds(PAD + chunk * CHUNK, CHUNK)],
                load_sems.at[kind * chunks + chunk],
            )
    small[0].start()
    for chunk in reversed(range(chunks)):
        loads[1, chunk].start()
        loads[2, chunk].start()
    small[1].start()
    for chunk in reversed(range(chunks)):
        loads[0, chunk].start()

    @pl.when(me == 0)
    def _():
        for raw in raws:
            raw[0:PAD] = jnp.zeros((PAD, raw.shape[1]), raw.dtype)

    small[0].wait()

    def halo(kind):
        return pltpu.make_async_remote_copy(
            src_ref=hbms[kind].at[pl.ds(tokens - 8, 8)],
            dst_ref=raws[kind].at[pl.ds(PAD - 8, 8)],
            send_sem=halo_send.at[kind],
            recv_sem=halo_recv.at[kind],
            device_id={"ctx": lax.rem(me + 1, n)},
            device_id_type=MESH,
        )

    def key_value(chunk):
        @pl.loop(0, heads)
        def _(head):
            lanes = pl.ds(pl.multiple_of(head * HDIM, HDIM), HDIM)
            half = conv_half(k_raw, [w_ref[1, tap : tap + 1, lanes] * 0.5 for tap in range(CONV)], chunk, lanes)
            key = (half + half * jnp.tanh(half)).astype(jnp.bfloat16)
            value = conv_half(v_raw, [w_ref[2, tap : tap + 1, lanes] for tap in range(CONV)], chunk, lanes).astype(jnp.bfloat16)
            k_feat[head, chunk] = key
            v_feat[head, chunk] = value
            states[chunk, head] = lax.dot_general(
                key, value, (((0,), (0,)), ((), ())), preferred_element_type=jnp.float32
            )

    for chunk in reversed(range(1, chunks)):
        if chunk == chunks - 1:
            loads[1, chunk].wait()
            loads[2, chunk].wait()
        loads[1, chunk - 1].wait()
        loads[2, chunk - 1].wait()
        key_value(chunk)

    pl.semaphore_wait(barrier, n - 1)

    @pl.when(me < n - 1)
    def _():
        for kind in (1, 2, 0):
            halo(kind).start()

    @pl.when(me > 0)
    def _():
        halo(1).wait_recv()
        halo(2).wait_recv()

    key_value(0)

    @pl.loop(0, heads)
    def _(head):
        total = states[0, head]
        for chunk in range(1, chunks):
            own = states[chunk, head]
            states[chunk, head] = total
            total = total + own
        send1[pl.ds(head * per_head, per_head)] = total.astype(jnp.bfloat16).reshape(per_head, piece, HDIM)

    def give(step):
        peer = lax.rem(me + step, n)
        return pltpu.make_async_remote_copy(
            src_ref=send1.at[peer], dst_ref=land1.at[me], send_sem=send1_sems.at[step], recv_sem=recv1_sems.at[me],
            device_id={"ctx": peer}, device_id_type=MESH,
        )

    def given(step):
        peer = lax.rem(me + n - step, n)
        return pltpu.make_async_remote_copy(
            src_ref=send1.at[peer], dst_ref=land1.at[peer], send_sem=send1_sems.at[step], recv_sem=recv1_sems.at[peer],
            device_id={"ctx": peer}, device_id_type=MESH,
        )

    def reply(step):
        peer = lax.rem(me + step, n)
        return pltpu.make_async_remote_copy(
            src_ref=send2.at[peer], dst_ref=land2.at[me], send_sem=send2_sems.at[step], recv_sem=recv2_sems.at[me],
            device_id={"ctx": peer}, device_id_type=MESH,
        )

    def replied(step):
        peer = lax.rem(me + n - step, n)
        return pltpu.make_async_remote_copy(
            src_ref=send2.at[peer], dst_ref=land2.at[peer], send_sem=send2_sems.at[step], recv_sem=recv2_sems.at[peer],
            device_id={"ctx": peer}, device_id_type=MESH,
        )

    order = sorted(range(1, n), key=lambda step: -min(step, n - step))
    for step in order:
        give(step).start()
    land1[me] = send1[me]

    small[1].wait()
    for chunk in range(chunks):
        loads[0, chunk].wait()

    @pl.when(me > 0)
    def _():
        halo(0).wait_recv()

    def query(chunk):
        @pl.loop(0, heads)
        def _(head):
            lanes = pl.ds(pl.multiple_of(head * HDIM, HDIM), HDIM)
            half = conv_half(q_raw, [w_ref[0, tap : tap + 1, lanes] * 0.5 for tap in range(CONV)], chunk, lanes)
            feat = ((half + half * jnp.tanh(half)) * HDIM ** (-0.5)).astype(jnp.bfloat16)
            q_feat[head, chunk] = feat
            scores = lax.dot_general(
                feat, k_feat[head, chunk], (((1,), (1,)), ((), ())), preferred_element_type=jnp.float32
            )
            row = lax.broadcasted_iota(jnp.int32, scores.shape, 0)
            col = lax.broadcasted_iota(jnp.int32, scores.shape, 1)
            scores = jnp.where(row >= col, scores, 0.0).astype(jnp.bfloat16)
            inner[head, chunk] = jnp.dot(scores, v_feat[head, chunk], preferred_element_type=jnp.float32)

    query(0)
    query(1)
    for step in order:
        given(step).wait_recv()
    total = jnp.zeros((piece, HDIM), jnp.float32)
    for block in range(n):
        send2[block] = total.astype(jnp.bfloat16)
        total = total + land1[block].astype(jnp.float32)
    for step in order:
        reply(step).start()
    land2[me] = send2[me]
    query(2)
    query(3)
    for step in order:
        replied(step).wait_recv()

    def finish(chunk):
        @pl.loop(0, heads)
        def _(head):
            lanes = pl.ds(pl.multiple_of(head * HDIM, HDIM), HDIM)
            prefix = land2[pl.ds(head * per_head, per_head)].reshape(HDIM, HDIM)
            if chunk:
                prefix = (prefix.astype(jnp.float32) + states[chunk, head]).astype(jnp.bfloat16)
            outputs = inner[head, chunk] + jnp.dot(q_feat[head, chunk], prefix, preferred_element_type=jnp.float32)
            scale_inv = lax.rsqrt(jnp.mean(outputs * outputs, axis=1, keepdims=True) + 1e-06)
            out_buf[pl.ds(chunk * CHUNK, CHUNK), lanes] = (outputs * scale_inv * g_ref[0:1, lanes]).astype(jnp.bfloat16)

        return pltpu.make_async_copy(
            out_buf.at[pl.ds(chunk * CHUNK, CHUNK)], out_hbm.at[pl.ds(chunk * CHUNK, CHUNK)], out_sems.at[chunk]
        )

    stores = []
    for chunk in range(chunks):
        store = finish(chunk)
        store.start()
        stores.append(store)

    @pl.when(me < n - 1)
    def _():
        for kind in range(3):
            halo(kind).wait_send()

    for step in order:
        give(step).wait_send()
        reply(step).wait_send()
    for store in stores:
        store.wait()


def body(queries, key_rows, value_rows, conv_weight, head_gain):
    tokens, width = queries.shape
    heads = width // HDIM
    n = lax.axis_size("ctx")
    chunks = tokens // CHUNK
    piece = heads * HDIM // n
    anywhere = pl.BlockSpec(memory_space=pl.ANY)
    bf16, f32 = jnp.bfloat16, jnp.float32
    dma = pltpu.SemaphoreType.DMA
    return pl.pallas_call(
        functools.partial(kernel, n, heads, tokens),
        out_shape=jax.ShapeDtypeStruct((tokens, width), bf16),
        in_specs=[anywhere] * 5,
        out_specs=anywhere,
        scratch_shapes=[
            *[pltpu.VMEM((tokens + PAD, width), bf16)] * 3,
            pltpu.VMEM((3, CONV, width), f32),
            pltpu.VMEM((1, width), f32),
            *[pltpu.VMEM((heads, chunks, CHUNK, HDIM), bf16)] * 3,
            pltpu.VMEM((heads, chunks, CHUNK, HDIM), f32),
            pltpu.VMEM((chunks, heads, HDIM, HDIM), f32),
            *[pltpu.VMEM((n, piece, HDIM), bf16)] * 4,
            pltpu.VMEM((tokens, width), bf16),
            dma((3 * chunks + 2,)), dma((3,)), dma((3,)),
            dma((n,)), dma((n,)), dma((n,)), dma((n,)),
            dma((chunks,)),
        ],
        compiler_params=pltpu.CompilerParams(
            collective_id=0, has_side_effects=True, vmem_limit_bytes=48 * 1024 * 1024
        ),
        name="linear_attention",
    )(queries, key_rows, value_rows, conv_weight, head_gain.reshape(1, width))


def solution(mesh):
    return jax.shard_map(
        body,
        mesh=mesh,
        in_specs=(
            P(("mp", "ctx"), None),
            P(("mp", "ctx"), None),
            P(("mp", "ctx"), None),
            P("mp", None, None),
            P("mp"),
        ),
        out_specs=P(("mp", "ctx"), None),
        check_vma=False,
    )
```

time: 611 us -> 49.4 us (0.08)
  the two profiles are of different devices: /device:TPU:128 before, /device:TPU:4 now
where the time goes in v1:
time: 49.4 us; the launch traced here: 49.2 us
  Pallas kernels  44.8 us (91%)
  local copies, waits for them, and re-layouts  4.4 us (9%)
    pallas_call x1, Pallas kernels, body(): pl.pallas_call(functools.partial(kernel, n, heads, tokens), out_shape=jax...  44.8 us
    unnamed x7, local copies, waits for them, and re-layouts  4.4 us

profile of v1, /device:TPU:4, one launch (start us, length us, event | category | flops | bytes accessed | tf_op | source)
XLA Modules:
  0.0 49.2 jit_solution(9320384599316544063)
XLA Ops:
  0.0 0.0 copy-start
  0.0 1.6 %copy-done = bf16[1024,1024]{1,0:T(8,128)(2,1)S(1)} copy-done((bf16[1024,1024]{1,0:T(8,128)(2,1)S(1)}, bf16[1024,1024]{1,0:T(8,128)(2,1)}, u32[]{:S(2)}) %copy-start) | copy-done | bytes 2097176
  1.6 0.0 copy-start.1
  1.6 0.8 %copy-done.1 = f32[3,4,1024]{2,1,0:T(4,128)S(1)} copy-done((f32[3,4,1024]{2,1,0:T(4,128)S(1)}, f32[3,4,1024]{2,1,0:T(4,128)}, u32[]{:S(2)}) %copy-start.1) | copy-done | bytes 49176
  2.4 0.0 copy-start.2
  2.4 0.7 %copy-done.2 = f32[1024]{0:T(1024)S(1)} copy-done((f32[1024]{0:T(1024)S(1)}, f32[1024]{0:T(1024)}, u32[]{:S(2)}) %copy-start.2) | copy-done | bytes 4120
  3.1 44.8 %linear_attention.1 = bf16[1024,1024]{1,0:T(8,128)(2,1)S(1)} custom-call(bf16[1024,1024]{1,0:T(8,128)(2,1)S(1)} %copy-done, bf16[1024,1024]{1,0:T(8,128)(2,1)} %k_hbm.1, bf16[1024,1024]{1,0:T(8,128)(2,1)} %v_hbm.1, f32[3,4,1024]{2,1,0:T(4,128)S(1)} %copy-done.1, f32[1,1024]{1,0:T(1,128)S(1)} %bitcast.1), custom_call_target="tpu_custom_call" | custom-call | tf_op jit(solution)/shard_map/linear_attention/pallas_call | solution.py:237
  47.9 1.3 %copy.7 = bf16[1024,1024]{1,0:T(8,128)(2,1)} copy(bf16[1024,1024]{1,0:T(8,128)(2,1)S(1)} %linear_attention.1) | data formatting | bytes 4194304
Async XLA Ops:
  0.0 1.6 %copy-start = (bf16[1024,1024]{1,0:T(8,128)(2,1)S(1)}, bf16[1024,1024]{1,0:T(8,128)(2,1)}, u32[]{:S(2)}) copy-start(bf16[1024,1024]{1,0:T(8,128)(2,1)} %q_hbm.1) | copy-start | bytes 6291460
  1.6 0.8 %copy-start.1 = (f32[3,4,1024]{2,1,0:T(4,128)S(1)}, f32[3,4,1024]{2,1,0:T(4,128)}, u32[]{:S(2)}) copy-start(f32[3,4,1024]{2,1,0:T(4,128)} %w_hbm.1) | copy-start | bytes 147460
  2.4 0.7 %copy-start.2 = (f32[1024]{0:T(1024)S(1)}, f32[1024]{0:T(1024)}, u32[]{:S(2)}) copy-start(f32[1024]{0:T(1024)} %param.9) | copy-start | bytes 12292

commit v2 on v1

--- a/solution.py
+++ b/solution.py
@@ -11,22 +11,21 @@
 CONV = 4
 PAD = 16
 CHUNK = 256
+KV_WIDE, Q_WIDE, OUT_WIDE = 4, 4, 4
 MESH = pl.DeviceIdType.MESH
 
 
-def conv_half(rows_ref, weights, chunk, lanes):
-    rows = rows_ref[pl.ds(pl.multiple_of(chunk * CHUNK, CHUNK), CHUNK + PAD), lanes].astype(jnp.float32)
-    back1 = pltpu.roll(rows, 1, 0)
-    late = weights[3] * rows + weights[2] * back1
-    early = weights[1] * rows + weights[0] * back1
-    return (late + pltpu.roll(early, 2, 0))[PAD:]
+def conv(rows_ref, wide, weights, chunk, lanes):
+    wide[...] = rows_ref[pl.ds(chunk * CHUNK, CHUNK + PAD), lanes].astype(jnp.float32)
+    terms = [weights[tap] * wide[pl.ds(PAD - CONV + 1 + tap, CHUNK)] for tap in range(CONV)]
+    return (terms[3] + terms[2]) + (terms[1] + terms[0])
 
 
 def kernel(
     n, heads, tokens,
     q_hbm, k_hbm, v_hbm, w_hbm, g_hbm, out_hbm,
     q_raw, k_raw, v_raw, w_ref, g_ref, q_feat, k_feat, v_feat,
-    inner, states, send1, land1, send2, land2, out_buf,
+    inner, states, send1, land1, send2, land2, out_buf, wide,
     load_sems, halo_send, halo_recv, send1_sems, recv1_sems, send2_sems, recv2_sems, out_sems,
 ):
     me = lax.axis_index("ctx")
@@ -76,18 +75,29 @@
             device_id_type=MESH,
         )
 
+    def several(count, width, one):
+        @pl.loop(0, count // width)
+        def _(turn):
+            for slot in range(width):
+                one(turn * width + slot, slot)
+
+    def lanes_of(head):
+        return pl.ds(pl.multiple_of(head * HDIM, HDIM), HDIM)
+
     def key_value(chunk):
-        @pl.loop(0, heads)
-        def _(head):
-            lanes = pl.ds(pl.multiple_of(head * HDIM, HDIM), HDIM)
-            half = conv_half(k_raw, [w_ref[1, tap : tap + 1, lanes] * 0.5 for tap in range(CONV)], chunk, lanes)
+        def one(head, slot):
+            lanes = lanes_of(head)
+            half = conv(k_raw, wide.at[2 * slot], [w_ref[1, tap : tap + 1, lanes] * 0.5 for tap in range(CONV)], chunk, lanes)
             key = (half + half * jnp.tanh(half)).astype(jnp.bfloat16)
-            value = conv_half(v_raw, [w_ref[2, tap : tap + 1, lanes] for tap in range(CONV)], chunk, lanes).astype(jnp.bfloat16)
+            taps = [w_ref[2, tap : tap + 1, lanes] for tap in range(CONV)]
+            value = conv(v_raw, wide.at[2 * slot + 1], taps, chunk, lanes).astype(jnp.bfloat16)
             k_feat[head, chunk] = key
             v_feat[head, chunk] = value
             states[chunk, head] = lax.dot_general(
                 key, value, (((0,), (0,)), ((), ())), preferred_element_type=jnp.float32
             )
+
+        several(heads, KV_WIDE, one)
 
     for chunk in reversed(range(1, chunks)):
         if chunk == chunks - 1:
@@ -162,10 +172,9 @@
         halo(0).wait_recv()
 
     def query(chunk):
-        @pl.loop(0, heads)
-        def _(head):
-            lanes = pl.ds(pl.multiple_of(head * HDIM, HDIM), HDIM)
-            half = conv_half(q_raw, [w_ref[0, tap : tap + 1, lanes] * 0.5 for tap in range(CONV)], chunk, lanes)
+        def one(head, slot):
+            lanes = lanes_of(head)
+            half = conv(q_raw, wide.at[slot], [w_ref[0, tap : tap + 1, lanes] * 0.5 for tap in range(CONV)], chunk, lanes)
             feat = ((half + half * jnp.tanh(half)) * HDIM ** (-0.5)).astype(jnp.bfloat16)
             q_feat[head, chunk] = feat
             scores = lax.dot_general(
@@ -176,6 +185,8 @@
             scores = jnp.where(row >= col, scores, 0.0).astype(jnp.bfloat16)
             inner[head, chunk] = jnp.dot(scores, v_feat[head, chunk], preferred_element_type=jnp.float32)
 
+        several(heads, Q_WIDE, one)
+
     query(0)
     query(1)
     for step in order:
@@ -193,9 +204,8 @@
         replied(step).wait_recv()
 
     def finish(chunk):
-        @pl.loop(0, heads)
-        def _(head):
-            lanes = pl.ds(pl.multiple_of(head * HDIM, HDIM), HDIM)
+        def one(head, slot):
+            lanes = lanes_of(head)
             prefix = land2[pl.ds(head * per_head, per_head)].reshape(HDIM, HDIM)
             if chunk:
                 prefix = (prefix.astype(jnp.float32) + states[chunk, head]).astype(jnp.bfloat16)
@@ -203,6 +213,7 @@
             scale_inv = lax.rsqrt(jnp.mean(outputs * outputs, axis=1, keepdims=True) + 1e-06)
             out_buf[pl.ds(chunk * CHUNK, CHUNK), lanes] = (outputs * scale_inv * g_ref[0:1, lanes]).astype(jnp.bfloat16)
 
+        several(heads, OUT_WIDE, one)
         return pltpu.make_async_copy(
             out_buf.at[pl.ds(chunk * CHUNK, CHUNK)], out_hbm.at[pl.ds(chunk * CHUNK, CHUNK)], out_sems.at[chunk]
         )
@@ -237,7 +248,7 @@
     return pl.pallas_call(
         functools.partial(kernel, n, heads, tokens),
         out_shape=jax.ShapeDtypeStruct((tokens, width), bf16),
-        in_specs=[anywhere] * 5,
+        in_specs=[pl.BlockSpec(memory_space=pltpu.HBM)] * 5,
         out_specs=anywhere,
         scratch_shapes=[
             *[pltpu.VMEM((tokens + PAD, width), bf16)] * 3,
@@ -248,6 +259,7 @@
             pltpu.VMEM((chunks, heads, HDIM, HDIM), f32),
             *[pltpu.VMEM((n, piece, HDIM), bf16)] * 4,
             pltpu.VMEM((tokens, width), bf16),
+            pltpu.VMEM((max(2 * KV_WIDE, Q_WIDE), CHUNK + PAD, HDIM), f32),
             dma((3 * chunks + 2,)), dma((3,)), dma((3,)),
             dma((n,)), dma((n,)), dma((n,)), dma((n,)),
             dma((chunks,)),
@@ -256,7 +268,7 @@
             collective_id=0, has_side_effects=True, vmem_limit_bytes=48 * 1024 * 1024
         ),
         name="linear_attention",
-    )(queries, key_rows, value_rows, conv_weight, head_gain.reshape(1, width))
+    )(*[pltpu.with_memory_space_constraint(x, pltpu.HBM) for x in (queries, key_rows, value_rows, conv_weight, head_gain.reshape(1, width))])
 
 
 def solution(mesh):

time: 49.4 us -> 38.4 us (0.78)
  the two profiles are of different devices: /device:TPU:4 before, /device:TPU:1 now
where the time goes in v2:
time: 38.4 us; the launch traced here: 38.3 us
  Pallas kernels  37 us (96%)
  local copies, waits for them, and re-layouts  1.32 us (3%)
    pallas_call x1, Pallas kernels, body(): pl.pallas_call(functools.partial(kernel, n, heads, tokens), out_shape=jax...  37 us
    unnamed x1, local copies, waits for them, and re-layouts  1.32 us

profile of v2, /device:TPU:1, one launch (start us, length us, event | category | flops | bytes accessed | tf_op | source)
XLA Modules:
  0.0 38.3 jit_solution(7689952543560159138)
XLA Ops:
  0.0 37.0 %linear_attention.1 = bf16[1024,1024]{1,0:T(8,128)(2,1)S(1)} custom-call(bf16[1024,1024]{1,0:T(8,128)(2,1)} %q_hbm.1, bf16[1024,1024]{1,0:T(8,128)(2,1)} %k_hbm.1, bf16[1024,1024]{1,0:T(8,128)(2,1)} %v_hbm.1, f32[3,4,1024]{2,1,0:T(4,128)} %w_hbm.1, f32[1,1024]{1,0:T(1,128)} %bitcast.1), custom_call_target="tpu_custom_call" | custom-call | tf_op jit(solution)/shard_map/linear_attention/pallas_call | solution.py:248
  37.0 1.3 %copy.7 = bf16[1024,1024]{1,0:T(8,128)(2,1)} copy(bf16[1024,1024]{1,0:T(8,128)(2,1)S(1)} %linear_attention.1) | data formatting | bytes 4194304

commit v3 on v0

v3 whole, which is shorter than its diff:
```python
import functools

import jax
import jax.numpy as jnp
from jax import lax
from jax.experimental import pallas as pl
from jax.experimental.pallas import tpu as pltpu
from jax.sharding import PartitionSpec as P

HDIM = 128
CONV = 4
PAD = 16
TAIL = 8
CHUNK = 256
MESH = pl.DeviceIdType.MESH


def conv(wide, weights, rows):
    terms = [weights[tap] * wide[pl.ds(PAD - CONV + 1 + tap, rows)] for tap in range(CONV)]
    return (terms[3] + terms[2]) + (terms[1] + terms[0])


def kernel(
    n, heads, tokens,
    q_hbm, k_hbm, v_hbm, w_hbm, g_hbm, out_hbm,
    q_raw, k_raw, v_raw, halo_k, halo_v, w_ref, g_ref, q_feat, k_feat, v_feat,
    inner, states, send1, land1, send2, land2, send3, land3, out_buf, wide,
    load_sems, halo_send, halo_recv, send1_sems, recv1_sems, send2_sems, recv2_sems, send3_sems, recv3_sems,
    ready_sems, out_sems,
):
    me = lax.axis_index("ctx")
    groups = n // heads
    group, member = me // heads, lax.rem(me, heads)
    chunks = tokens // CHUNK
    bf16, f32 = jnp.bfloat16, jnp.float32

    def mate(step):
        return group * heads + lax.rem(member + step, heads)

    barrier = pltpu.get_barrier_semaphore()

    def greet(peer):
        pl.semaphore_signal(barrier, inc=1, device_id={"ctx": peer}, device_id_type=MESH)

    for step in range(1, heads):
        greet(mate(step))
    for other in range(1, groups):
        @pl.when(group < other)
        def _():
            greet(other * heads + member)

    @pl.when(jnp.logical_and(member == 0, group > 0))
    def _():
        greet(me - 1)

    w_load = pltpu.make_async_copy(w_hbm, w_ref, load_sems.at[3, 0])
    g_load = pltpu.make_async_copy(g_hbm, g_ref, load_sems.at[3, 1])

    def load(kind, chunk):
        rows = chunk * CHUNK
        return pltpu.make_async_copy(
            (q_hbm, k_hbm, v_hbm)[kind].at[pl.ds(rows, CHUNK)],
            (q_raw, k_raw, v_raw)[kind].at[pl.ds(PAD + rows, CHUNK)],
            load_sems.at[kind, chunk],
        )

    w_load.start()
    for chunk in range(chunks):
        load(1, chunk).start()
        load(2, chunk).start()
    g_load.start()
    for chunk in range(chunks):
        load(0, chunk).start()

    k_raw[0:PAD] = jnp.zeros((PAD, heads * HDIM), bf16)
    v_raw[0:PAD] = jnp.zeros((PAD, heads * HDIM), bf16)

    @pl.when(me == 0)
    def _():
        q_raw[0:PAD] = jnp.zeros((PAD, heads * HDIM), bf16)
        halo_k[...] = jnp.zeros((TAIL, heads * HDIM), bf16)
        halo_v[...] = jnp.zeros((TAIL, heads * HDIM), bf16)

    for other in range(groups - 1):
        @pl.when(group <= other)
        def _():
            land3[other] = jnp.zeros((HDIM, HDIM), bf16)

    def halo(kind):
        return pltpu.make_async_remote_copy(
            src_ref=(q_hbm, k_hbm, v_hbm)[kind].at[pl.ds(tokens - TAIL, TAIL)],
            dst_ref=(q_raw.at[pl.ds(PAD - TAIL, TAIL)], halo_k, halo_v)[kind],
            send_sem=halo_send.at[kind],
            recv_sem=halo_recv.at[kind],
            device_id={"ctx": lax.rem(me + 1, n)},
            device_id_type=MESH,
        )

    def lanes_of(head):
        return pl.ds(head * HDIM, HDIM)

    def taps(kind, head, factor=None):
        weights = [w_ref[kind, tap : tap + 1, lanes_of(head)] for tap in range(CONV)]
        return weights if factor is None else [weight * factor for weight in weights]

    def silu(half):
        return half + half * jnp.tanh(half)

    def outer(key, value):
        return lax.dot_general(key, value, (((0,), (0,)), ((), ())), preferred_element_type=f32)

    w_load.wait()

    @pl.loop(0, chunks)
    def _(chunk):
        load(1, chunk).wait()
        load(2, chunk).wait()
        rows = pl.ds(pl.multiple_of(chunk * CHUNK, CHUNK), CHUNK + PAD)
        for head in range(heads):
            wide[2 * head] = k_raw[rows, lanes_of(head)].astype(f32)
            key = silu(conv(wide.at[2 * head], taps(1, head, 0.5), CHUNK)).astype(bf16)
            wide[2 * head + 1] = v_raw[rows, lanes_of(head)].astype(f32)
            value = conv(wide.at[2 * head + 1], taps(2, head), CHUNK).astype(bf16)
            k_feat[head, chunk] = key
            v_feat[head, chunk] = value
            states[chunk, head] = outer(key, value)

    waits = heads - 1 + group + jnp.logical_and(member == heads - 1, group < groups - 1).astype(jnp.int32)
    pl.semaphore_wait(barrier, waits)

    @pl.when(me < n - 1)
    def _():
        for kind in (1, 2, 0):
            halo(kind).start()

    for other in range(groups - 1):
        @pl.when(group > other)
        def _():
            pl.semaphore_signal(
                ready_sems.at[group], inc=1, device_id={"ctx": other * heads + member}, device_id_type=MESH
            )

    @pl.when(me > 0)
    def _():
        halo(1).wait_recv()
        halo(2).wait_recv()

    for head in range(heads):
        new = []
        for kind, raw, tail in ((1, k_raw, halo_k), (2, v_raw, halo_v)):
            slot = wide.at[2 * head + kind - 1]
            slot[PAD - TAIL : PAD] = tail[:, lanes_of(head)].astype(f32)
            slot[PAD : 2 * PAD] = raw[PAD : 2 * PAD, lanes_of(head)].astype(f32)
            new.append(conv(slot, taps(kind, head, 0.5 if kind == 1 else None), PAD))
        key, value = silu(new[0]).astype(bf16), new[1].astype(bf16)
        old_key, old_value = k_feat[head, 0, 0:PAD], v_feat[head, 0, 0:PAD]
        k_feat[head, 0, 0:PAD] = key
        v_feat[head, 0, 0:PAD] = value
        total = states[0, head] + outer(
            jnp.concatenate([key, old_key], axis=0), jnp.concatenate([value, -old_value], axis=0)
        )
        states[0, head] = jnp.zeros((HDIM, HDIM), f32)
        for chunk in range(1, chunks):
            own = states[chunk, head]
            states[chunk, head] = total
            total = total + own
        send1[head] = total.astype(bf16)

    def exchange(src, dst, send_sems, recv_sems, step):
        peer = mate(step)
        return pltpu.make_async_remote_copy(
            src_ref=src.at[lax.rem(member + step, heads)], dst_ref=dst.at[member],
            send_sem=send_sems.at[step], recv_sem=recv_sems.at[member],
            device_id={"ctx": peer}, device_id_type=MESH,
        )

    def arrival(src, dst, send_sems, recv_sems, step):
        source = lax.rem(member + heads - step, heads)
        return pltpu.make_async_remote_copy(
            src_ref=src.at[source], dst_ref=dst.at[source],
            send_sem=send_sems.at[step], recv_sem=recv_sems.at[source],
            device_id={"ctx": mate(step)}, device_id_type=MESH,
        )

    first = (send1, land1, send1_sems, recv1_sems)
    second = (send2, land2, send2_sems, recv2_sems)
    order = sorted(range(1, heads), key=lambda step: -min(step, heads - step))
    for step in order:
        exchange(*first, step).start()
    land1[member] = send1[member]

    g_load.wait()
    for chunk in range(chunks):
        load(0, chunk).wait()

    @pl.when(me > 0)
    def _():
        halo(0).wait_recv()

    @pl.loop(0, chunks)
    def _(chunk):
        rows = pl.ds(pl.multiple_of(chunk * CHUNK, CHUNK), CHUNK + PAD)
        row = lax.broadcasted_iota(jnp.int32, (CHUNK, CHUNK), 0)
        col = lax.broadcasted_iota(jnp.int32, (CHUNK, CHUNK), 1)
        for head in range(heads):
            wide[head] = q_raw[rows, lanes_of(head)].astype(f32)
            feat = (silu(conv(wide.at[head], taps(0, head, 0.5), CHUNK)) * HDIM ** (-0.5)).astype(bf16)
            q_feat[head, chunk] = feat
            scores = lax.dot_general(
                feat, k_feat[head, chunk], (((1,), (1,)), ((), ())), preferred_element_type=f32
            )
            scores = jnp.where(row >= col, scores, 0.0).astype(bf16)
            inner[head, chunk] = jnp.dot(scores, v_feat[head, chunk], preferred_element_type=f32)

    for step in order:
        arrival(*first, step).wait_recv()
    total = land1[0].astype(f32)
    for source in range(1, heads):
        total = total + land1[source].astype(f32)
    send3[...] = total.astype(bf16)

    def onward(other):
        return pltpu.make_async_remote_copy(
            src_ref=send3, dst_ref=land3.at[group], send_sem=send3_sems.at[other], recv_sem=recv3_sems.at[group],
            device_id={"ctx": other * heads + member}, device_id_type=MESH,
        )

    def upstream(other):
        return pltpu.make_async_remote_copy(
            src_ref=send3, dst_ref=land3.at[other], send_sem=send3_sems.at[other], recv_sem=recv3_sems.at[other],
            device_id={"ctx": lax.rem(me + heads, n)}, device_id_type=MESH,
        )

    for other in range(1, groups):
        @pl.when(group < other)
        def _():
            pl.semaphore_wait(ready_sems.at[other], 1)
            onward(other).start()
    for other in range(groups - 1):
        @pl.when(group > other)
        def _():
            upstream(other).wait_recv()

    total = land3[0].astype(f32)
    for other in range(1, groups - 1):
        total = total + land3[other].astype(f32)
    for source in range(heads):
        send2[source] = total.astype(bf16)
        total = total + land1[source].astype(f32)
    for step in order:
        exchange(*second, step).start()
    land2[member] = send2[member]
    for step in order:
        arrival(*second, step).wait_recv()

    def store(chunk):
        rows = pl.ds(pl.multiple_of(chunk * CHUNK, CHUNK), CHUNK)
        return pltpu.make_async_copy(out_buf.at[rows], out_hbm.at[rows], out_sems.at[chunk])

    @pl.loop(0, chunks)
    def _(chunk):
        rows = pl.ds(pl.multiple_of(chunk * CHUNK, CHUNK), CHUNK)
        ones = jnp.full((HDIM, HDIM), 1 / HDIM, bf16)
        for head in range(heads):
            prefix = (land2[head].astype(f32) + states[chunk, head]).astype(bf16)
            outputs = inner[head, chunk] + jnp.dot(q_feat[head, chunk], prefix, preferred_element_type=f32)
            mean = jnp.dot((outputs * outputs).astype(bf16), ones, preferred_element_type=f32)
            scaled = outputs * lax.rsqrt(mean + 1e-06) * g_ref[0:1, lanes_of(head)]
            out_buf[rows, lanes_of(head)] = scaled.astype(bf16)
        store(chunk).start()

    @pl.when(me < n - 1)
    def _():
        for kind in range(3):
            halo(kind).wait_send()

    for step in order:
        exchange(*first, step).wait_send()
        exchange(*second, step).wait_send()
    for other in range(1, groups):
        @pl.when(group < other)
        def _():
            onward(other).wait_send()
    for chunk in range(chunks):
        store(chunk).wait()


def body(queries, key_rows, value_rows, conv_weight, head_gain):
    tokens, width = queries.shape
    heads = width // HDIM
    n = lax.axis_size("ctx")
    groups = n // heads
    chunks = tokens // CHUNK
    bf16, f32 = jnp.bfloat16, jnp.float32
    dma = pltpu.SemaphoreType.DMA
    operands = (queries, key_rows, value_rows, conv_weight, head_gain.reshape(1, width))
    return pl.pallas_call(
        functools.partial(kernel, n, heads, tokens),
        out_shape=jax.ShapeDtypeStruct((tokens, width), bf16),
        in_specs=[pl.BlockSpec(memory_space=pltpu.HBM)] * 5,
        out_specs=pl.BlockSpec(memory_space=pl.ANY),
        scratch_shapes=[
            *[pltpu.VMEM((tokens + PAD, width), bf16)] * 3,
            *[pltpu.VMEM((TAIL, width), bf16)] * 2,
            pltpu.VMEM((3, CONV, width), f32),
            pltpu.VMEM((1, width), f32),
            *[pltpu.VMEM((heads, chunks, CHUNK, HDIM), bf16)] * 3,
            pltpu.VMEM((heads, chunks, CHUNK, HDIM), f32),
            pltpu.VMEM((chunks, heads, HDIM, HDIM), f32),
            *[pltpu.VMEM((heads, HDIM, HDIM), bf16)] * 4,
            pltpu.VMEM((HDIM, HDIM), bf16),
            pltpu.VMEM((groups - 1, HDIM, HDIM), bf16),
            pltpu.VMEM((tokens, width), bf16),
            pltpu.VMEM((2 * heads, CHUNK + PAD, HDIM), f32),
            dma((4, chunks)), dma((3,)), dma((3,)),
            dma((heads,)), dma((heads,)), dma((heads,)), dma((heads,)), dma((groups,)), dma((groups,)),
            pltpu.SemaphoreType.REGULAR((groups,)), dma((chunks,)),
        ],
        compiler_params=pltpu.CompilerParams(
            collective_id=0, has_side_effects=True, vmem_limit_bytes=48 * 1024 * 1024
        ),
        name="linear_attention",
    )(*[pltpu.with_memory_space_constraint(x, pltpu.HBM) for x in operands])


def solution(mesh):
    return jax.shard_map(
        body,
        mesh=mesh,
        in_specs=(
            P(("mp", "ctx"), None),
            P(("mp", "ctx"), None),
            P(("mp", "ctx"), None),
            P("mp", None, None),
            P("mp"),
        ),
        out_specs=P(("mp", "ctx"), None),
        check_vma=False,
    )
```

time: 611 us -> 29.9 us (0.05)
  the two profiles are of different devices: /device:TPU:128 before, /device:TPU:230 now
where the time goes in v3:
time: 29.9 us; the launch traced here: 29.8 us
  Pallas kernels  28.5 us (95%)
  local copies, waits for them, and re-layouts  1.32 us (4%)
    pallas_call x1, Pallas kernels, body(): pl.pallas_call(functools.partial(kernel, n, heads, tokens), out_shape=jax...  28.5 us
    unnamed x1, local copies, waits for them, and re-layouts  1.32 us

profile of v3, /device:TPU:230, one launch (start us, length us, event | category | flops | bytes accessed | tf_op | source)
XLA Modules:
  0.0 29.8 jit_solution(7272548312384431583)
XLA Ops:
  0.0 28.5 %linear_attention.1 = bf16[1024,1024]{1,0:T(8,128)(2,1)S(1)} custom-call(bf16[1024,1024]{1,0:T(8,128)(2,1)} %q_hbm.1, bf16[1024,1024]{1,0:T(8,128)(2,1)} %k_hbm.1, bf16[1024,1024]{1,0:T(8,128)(2,1)} %v_hbm.1, f32[3,4,1024]{2,1,0:T(4,128)} %w_hbm.1, f32[1,1024]{1,0:T(1,128)} %bitcast.1), custom_call_target="tpu_custom_call" | custom-call | tf_op jit(solution)/shard_map/linear_attention/pallas_call | solution.py:297
  28.5 1.3 %copy.7 = bf16[1024,1024]{1,0:T(8,128)(2,1)} copy(bf16[1024,1024]{1,0:T(8,128)(2,1)S(1)} %linear_attention.1) | data formatting | bytes 4194304

commit v4 on v3

--- a/solution.py
+++ b/solution.py
@@ -12,6 +12,7 @@
 PAD = 16
 TAIL = 8
 CHUNK = 256
+HALO_AT = 1
 MESH = pl.DeviceIdType.MESH
 
 
@@ -22,11 +23,11 @@
 
 def kernel(
     n, heads, tokens,
-    q_hbm, k_hbm, v_hbm, w_hbm, g_hbm, out_hbm,
+    q_hbm, k_hbm, v_hbm, w_hbm, g_hbm, out_ref,
     q_raw, k_raw, v_raw, halo_k, halo_v, w_ref, g_ref, q_feat, k_feat, v_feat,
-    inner, states, send1, land1, send2, land2, send3, land3, out_buf, wide,
+    inner, states, send1, land1, send2, land2, send3, land3, wide,
     load_sems, halo_send, halo_recv, send1_sems, recv1_sems, send2_sems, recv2_sems, send3_sems, recv3_sems,
-    ready_sems, out_sems,
+    ready_sems,
 ):
     me = lax.axis_index("ctx")
     groups = n // heads
@@ -109,10 +110,30 @@
     def outer(key, value):
         return lax.dot_general(key, value, (((0,), (0,)), ((), ())), preferred_element_type=f32)
 
+    def meet():
+        waits = heads - 1 + group + jnp.logical_and(member == heads - 1, group < groups - 1).astype(jnp.int32)
+        pl.semaphore_wait(barrier, waits)
+
+        @pl.when(me < n - 1)
+        def _():
+            for kind in (1, 2, 0):
+                halo(kind).start()
+
+        for other in range(groups - 1):
+            @pl.when(group > other)
+            def _():
+                pl.semaphore_signal(
+                    ready_sems.at[group], inc=1, device_id={"ctx": other * heads + member}, device_id_type=MESH
+                )
+
     w_load.wait()
 
     @pl.loop(0, chunks)
     def _(chunk):
+        @pl.when(chunk == HALO_AT)
+        def _():
+            meet()
+
         load(1, chunk).wait()
         load(2, chunk).wait()
         rows = pl.ds(pl.multiple_of(chunk * CHUNK, CHUNK), CHUNK + PAD)
@@ -124,21 +145,6 @@
             k_feat[head, chunk] = key
             v_feat[head, chunk] = value
             states[chunk, head] = outer(key, value)
-
-    waits = heads - 1 + group + jnp.logical_and(member == heads - 1, group < groups - 1).astype(jnp.int32)
-    pl.semaphore_wait(barrier, waits)
-
-    @pl.when(me < n - 1)
-    def _():
-        for kind in (1, 2, 0):
-            halo(kind).start()
-
-    for other in range(groups - 1):
-        @pl.when(group > other)
-        def _():
-            pl.semaphore_signal(
-                ready_sems.at[group], inc=1, device_id={"ctx": other * heads + member}, device_id_type=MESH
-            )
 
     @pl.when(me > 0)
     def _():
@@ -184,7 +190,7 @@
 
     first = (send1, land1, send1_sems, recv1_sems)
     second = (send2, land2, send2_sems, recv2_sems)
-    order = sorted(range(1, heads), key=lambda step: -min(step, heads - step))
+    order = sorted(range(1, heads), key=lambda step: min(step, heads - step))
     for step in order:
         exchange(*first, step).start()
     land1[member] = send1[member]
@@ -250,24 +256,24 @@
     for step in order:
         exchange(*second, step).start()
     land2[member] = send2[member]
+    ones = jnp.full((HDIM, HDIM), 1 / HDIM, bf16)
+
+    def finish(head):
+        lanes = pl.ds(pl.multiple_of(head * HDIM, HDIM), HDIM)
+        gain = g_ref[0:1, lanes]
+        prefix = land2[head].astype(f32)
+        for chunk in range(chunks):
+            outputs = inner[head, chunk] + jnp.dot(
+                q_feat[head, chunk], (prefix + states[chunk, head]).astype(bf16), preferred_element_type=f32
+            )
+            mean = jnp.dot((outputs * outputs).astype(bf16), ones, preferred_element_type=f32)
+            scaled = outputs * lax.rsqrt(mean + 1e-06) * gain
+            out_ref[pl.ds(chunk * CHUNK, CHUNK), lanes] = scaled.astype(bf16)
+
+    finish(member)
     for step in order:
         arrival(*second, step).wait_recv()
-
-    def store(chunk):
-        rows = pl.ds(pl.multiple_of(chunk * CHUNK, CHUNK), CHUNK)
-        return pltpu.make_async_copy(out_buf.at[rows], out_hbm.at[rows], out_sems.at[chunk])
-
-    @pl.loop(0, chunks)
-    def _(chunk):
-        rows = pl.ds(pl.multiple_of(chunk * CHUNK, CHUNK), CHUNK)
-        ones = jnp.full((HDIM, HDIM), 1 / HDIM, bf16)
-        for head in range(heads):
-            prefix = (land2[head].astype(f32) + states[chunk, head]).astype(bf16)
-            outputs = inner[head, chunk] + jnp.dot(q_feat[head, chunk], prefix, preferred_element_type=f32)
-            mean = jnp.dot((outputs * outputs).astype(bf16), ones, preferred_element_type=f32)
-            scaled = outputs * lax.rsqrt(mean + 1e-06) * g_ref[0:1, lanes_of(head)]
-            out_buf[rows, lanes_of(head)] = scaled.astype(bf16)
-        store(chunk).start()
+        finish(lax.rem(member + heads - step, heads))
 
     @pl.when(me < n - 1)
     def _():
@@ -281,8 +287,6 @@
         @pl.when(group < other)
         def _():
             onward(other).wait_send()
-    for chunk in range(chunks):
-        store(chunk).wait()
 
 
 def body(queries, key_rows, value_rows, conv_weight, head_gain):
@@ -298,7 +302,7 @@
         functools.partial(kernel, n, heads, tokens),
         out_shape=jax.ShapeDtypeStruct((tokens, width), bf16),
         in_specs=[pl.BlockSpec(memory_space=pltpu.HBM)] * 5,
-        out_specs=pl.BlockSpec(memory_space=pl.ANY),
+        out_specs=pl.BlockSpec(memory_space=pltpu.VMEM),
         scratch_shapes=[
             *[pltpu.VMEM((tokens + PAD, width), bf16)] * 3,
             *[pltpu.VMEM((TAIL, width), bf16)] * 2,
@@ -310,11 +314,10 @@
             *[pltpu.VMEM((heads, HDIM, HDIM), bf16)] * 4,
             pltpu.VMEM((HDIM, HDIM), bf16),
             pltpu.VMEM((groups - 1, HDIM, HDIM), bf16),
-            pltpu.VMEM((tokens, width), bf16),
             pltpu.VMEM((2 * heads, CHUNK + PAD, HDIM), f32),
             dma((4, chunks)), dma((3,)), dma((3,)),
             dma((heads,)), dma((heads,)), dma((heads,)), dma((heads,)), dma((groups,)), dma((groups,)),
-            pltpu.SemaphoreType.REGULAR((groups,)), dma((chunks,)),
+            pltpu.SemaphoreType.REGULAR((groups,)),
         ],
         compiler_params=pltpu.CompilerParams(
             collective_id=0, has_side_effects=True, vmem_limit_bytes=48 * 1024 * 1024

time: 29.9 us -> 25.8 us (0.86)
  Pallas kernels: 28.5 us -> 24.4 us
    pallas_call x1, Pallas kernels: 28.5 us -> 24.4 us  [body(): pl.pallas_call(functools.partial(kernel, n, heads, tokens), out_shape=jax...]
where the time goes in v4:
time: 25.8 us
  Pallas kernels  24.4 us (95%)
  local copies, waits for them, and re-layouts  1.32 us (5%)
    pallas_call x1, Pallas kernels, body(): pl.pallas_call(functools.partial(kernel, n, heads, tokens), out_shape=jax...  24.4 us
    unnamed x1, local copies, waits for them, and re-layouts  1.32 us

profile of v4, /device:TPU:230, one launch (start us, length us, event | category | flops | bytes accessed | tf_op | source)
XLA Modules:
  0.0 25.8 jit_solution(6011830328137326032)
XLA Ops:
  0.0 24.4 %linear_attention.1 = bf16[1024,1024]{1,0:T(8,128)(2,1)S(1)} custom-call(bf16[1024,1024]{1,0:T(8,128)(2,1)} %q_hbm.1, bf16[1024,1024]{1,0:T(8,128)(2,1)} %k_hbm.1, bf16[1024,1024]{1,0:T(8,128)(2,1)} %v_hbm.1, f32[3,4,1024]{2,1,0:T(4,128)} %w_hbm.1, f32[1,1024]{1,0:T(1,128)} %bitcast.1), custom_call_target="tpu_custom_call" | custom-call | tf_op jit(solution)/shard_map/linear_attention/pallas_call | solution.py:301
  24.4 1.3 %copy.7 = bf16[1024,1024]{1,0:T(8,128)(2,1)} copy(bf16[1024,1024]{1,0:T(8,128)(2,1)S(1)} %linear_attention.1) | data formatting | bytes 4194304

commit v5 on v4

--- a/solution.py
+++ b/solution.py
@@ -25,7 +25,7 @@
     n, heads, tokens,
     q_hbm, k_hbm, v_hbm, w_hbm, g_hbm, out_ref,
     q_raw, k_raw, v_raw, halo_k, halo_v, w_ref, g_ref, q_feat, k_feat, v_feat,
-    inner, states, send1, land1, send2, land2, send3, land3, wide,
+    inner, states, whole0, whole1, squares0, squares1, send1, land1, send2, land2, send3, land3, wide,
     load_sems, halo_send, halo_recv, send1_sems, recv1_sems, send2_sems, recv2_sems, send3_sems, recv3_sems,
     ready_sems,
 ):
@@ -34,9 +34,18 @@
     group, member = me // heads, lax.rem(me, heads)
     chunks = tokens // CHUNK
     bf16, f32 = jnp.bfloat16, jnp.float32
-
-    def mate(step):
-        return group * heads + lax.rem(member + step, heads)
+    whole, squares = (whole0, whole1), (squares0, squares1)
+
+    def partner(mask):
+        found, bit = member, 1
+        while bit < heads:
+            if mask & bit:
+                found = found + bit * (1 - 2 * lax.rem(member // bit, 2))
+            bit *= 2
+        return found
+
+    def mate(mask):
+        return group * heads + partner(mask)
 
     barrier = pltpu.get_barrier_semaphore()
 
@@ -175,13 +184,13 @@
     def exchange(src, dst, send_sems, recv_sems, step):
         peer = mate(step)
         return pltpu.make_async_remote_copy(
-            src_ref=src.at[lax.rem(member + step, heads)], dst_ref=dst.at[member],
+            src_ref=src.at[partner(step)], dst_ref=dst.at[member],
             send_sem=send_sems.at[step], recv_sem=recv_sems.at[member],
             device_id={"ctx": peer}, device_id_type=MESH,
         )
 
     def arrival(src, dst, send_sems, recv_sems, step):
-        source = lax.rem(member + heads - step, heads)
+        source = partner(step)
         return pltpu.make_async_remote_copy(
             src_ref=src.at[source], dst_ref=dst.at[source],
             send_sem=send_sems.at[step], recv_sem=recv_sems.at[source],
@@ -190,7 +199,7 @@
 
     first = (send1, land1, send1_sems, recv1_sems)
     second = (send2, land2, send2_sems, recv2_sems)
-    order = sorted(range(1, heads), key=lambda step: min(step, heads - step))
+    order = [1, 3, 4, 2, 5, 7, 6]
     for step in order:
         exchange(*first, step).start()
     land1[member] = send1[member]
@@ -258,22 +267,31 @@
     land2[member] = send2[member]
     ones = jnp.full((HDIM, HDIM), 1 / HDIM, bf16)
 
-    def finish(head):
-        lanes = pl.ds(pl.multiple_of(head * HDIM, HDIM), HDIM)
-        gain = g_ref[0:1, lanes]
+    def add_prefix(head, place):
         prefix = land2[head].astype(f32)
         for chunk in range(chunks):
             outputs = inner[head, chunk] + jnp.dot(
                 q_feat[head, chunk], (prefix + states[chunk, head]).astype(bf16), preferred_element_type=f32
             )
-            mean = jnp.dot((outputs * outputs).astype(bf16), ones, preferred_element_type=f32)
-            scaled = outputs * lax.rsqrt(mean + 1e-06) * gain
+            whole[place % 2][chunk] = outputs
+            squares[place % 2][chunk] = (outputs * outputs).astype(bf16)
+
+    def norm(head, place):
+        lanes = pl.ds(pl.multiple_of(head * HDIM, HDIM), HDIM)
+        gain = g_ref[0:1, lanes]
+        for chunk in range(chunks):
+            mean = jnp.dot(squares[place % 2][chunk], ones, preferred_element_type=f32)
+            scaled = whole[place % 2][chunk] * lax.rsqrt(mean + 1e-06) * gain
             out_ref[pl.ds(chunk * CHUNK, CHUNK), lanes] = scaled.astype(bf16)
 
-    finish(member)
-    for step in order:
+    add_prefix(member, 0)
+    last = member
+    for place, step in enumerate(order):
         arrival(*second, step).wait_recv()
-        finish(lax.rem(member + heads - step, heads))
+        add_prefix(partner(step), place + 1)
+        norm(last, place)
+        last = partner(step)
+    norm(last, len(order))
 
     @pl.when(me < n - 1)
     def _():
@@ -311,6 +329,8 @@
             *[pltpu.VMEM((heads, chunks, CHUNK, HDIM), bf16)] * 3,
             pltpu.VMEM((heads, chunks, CHUNK, HDIM), f32),
             pltpu.VMEM((chunks, heads, HDIM, HDIM), f32),
+            *[pltpu.VMEM((chunks, CHUNK, HDIM), f32)] * 2,
+            *[pltpu.VMEM((chunks, CHUNK, HDIM), bf16)] * 2,
             *[pltpu.VMEM((heads, HDIM, HDIM), bf16)] * 4,
             pltpu.VMEM((HDIM, HDIM), bf16),
             pltpu.VMEM((groups - 1, HDIM, HDIM), bf16),

time: 25.8 us -> 25.3 us (0.981); the launches traced: 25.8 us -> 24.8 us
  Pallas kernels: 24.4 us -> 23.5 us
    pallas_call x1, Pallas kernels: 24.4 us -> 23.5 us  [body(): pl.pallas_call(functools.partial(kernel, n, heads, tokens), out_shape=jax...]
where the time goes in v5:
time: 25.3 us; the launch traced here: 24.8 us
  Pallas kernels  23.5 us (93%)
  local copies, waits for them, and re-layouts  1.32 us (5%)
    pallas_call x1, Pallas kernels, body(): pl.pallas_call(functools.partial(kernel, n, heads, tokens), out_shape=jax...  23.5 us
    unnamed x1, local copies, waits for them, and re-layouts  1.32 us

profile of v5, /device:TPU:230, one launch (start us, length us, event | category | flops | bytes accessed | tf_op | source)
XLA Modules:
  0.0 24.8 jit_solution(8225098294561111071)
XLA Ops:
  0.0 23.5 %linear_attention.1 = bf16[1024,1024]{1,0:T(8,128)(2,1)S(1)} custom-call(bf16[1024,1024]{1,0:T(8,128)(2,1)} %q_hbm.1, bf16[1024,1024]{1,0:T(8,128)(2,1)} %k_hbm.1, bf16[1024,1024]{1,0:T(8,128)(2,1)} %v_hbm.1, f32[3,4,1024]{2,1,0:T(4,128)} %w_hbm.1, f32[1,1024]{1,0:T(1,128)} %bitcast.1), custom_call_target="tpu_custom_call" | custom-call | tf_op jit(solution)/shard_map/linear_attention/pallas_call | solution.py:319
  23.5 1.3 %copy.7 = bf16[1024,1024]{1,0:T(8,128)(2,1)} copy(bf16[1024,1024]{1,0:T(8,128)(2,1)S(1)} %linear_attention.1) | data formatting | bytes 4194304

commit v6 on v5

--- a/solution.py
+++ b/solution.py
@@ -47,22 +47,6 @@
     def mate(mask):
         return group * heads + partner(mask)
 
-    barrier = pltpu.get_barrier_semaphore()
-
-    def greet(peer):
-        pl.semaphore_signal(barrier, inc=1, device_id={"ctx": peer}, device_id_type=MESH)
-
-    for step in range(1, heads):
-        greet(mate(step))
-    for other in range(1, groups):
-        @pl.when(group < other)
-        def _():
-            greet(other * heads + member)
-
-    @pl.when(jnp.logical_and(member == 0, group > 0))
-    def _():
-        greet(me - 1)
-
     w_load = pltpu.make_async_copy(w_hbm, w_ref, load_sems.at[3, 0])
     g_load = pltpu.make_async_copy(g_hbm, g_ref, load_sems.at[3, 1])
 
@@ -75,7 +59,26 @@
         )
 
     w_load.start()
-    for chunk in range(chunks):
+    load(1, 0).start()
+    load(2, 0).start()
+
+    barrier = pltpu.get_barrier_semaphore()
+
+    def greet(peer):
+        pl.semaphore_signal(barrier, inc=1, device_id={"ctx": peer}, device_id_type=MESH)
+
+    for step in range(1, heads):
+        greet(mate(step))
+    for other in range(1, groups):
+        @pl.when(group < other)
+        def _():
+            greet(other * heads + member)
+
+    @pl.when(jnp.logical_and(member == 0, group > 0))
+    def _():
+        greet(me - 1)
+
+    for chunk in range(1, chunks):
         load(1, chunk).start()
         load(2, chunk).start()
     g_load.start()

time: 25.3 us -> 25.3 us (level)
  no operation moved by 1% of the time
where the time goes in v6:
time: 25.3 us; the launch traced here: 24.8 us
  Pallas kernels  23.5 us (93%)
  local copies, waits for them, and re-layouts  1.32 us (5%)
    pallas_call x1, Pallas kernels, body(): pl.pallas_call(functools.partial(kernel, n, heads, tokens), out_shape=jax...  23.5 us
    unnamed x1, local copies, waits for them, and re-layouts  1.32 us

profile of v6, /device:TPU:230, one launch (start us, length us, event | category | flops | bytes accessed | tf_op | source)
XLA Modules:
  0.0 24.8 jit_solution(13495369760390348058)
XLA Ops:
  0.0 23.5 %linear_attention.1 = bf16[1024,1024]{1,0:T(8,128)(2,1)S(1)} custom-call(bf16[1024,1024]{1,0:T(8,128)(2,1)} %q_hbm.1, bf16[1024,1024]{1,0:T(8,128)(2,1)} %k_hbm.1, bf16[1024,1024]{1,0:T(8,128)(2,1)} %v_hbm.1, f32[3,4,1024]{2,1,0:T(4,128)} %w_hbm.1, f32[1,1024]{1,0:T(1,128)} %bitcast.1), custom_call_target="tpu_custom_call" | custom-call | tf_op jit(solution)/shard_map/linear_attention/pallas_call | solution.py:322
  23.5 1.3 %copy.7 = bf16[1024,1024]{1,0:T(8,128)(2,1)} copy(bf16[1024,1024]{1,0:T(8,128)(2,1)S(1)} %linear_attention.1) | data formatting | bytes 4194304

commit v7 on v5

--- a/solution.py
+++ b/solution.py
@@ -285,11 +285,13 @@
             out_ref[pl.ds(chunk * CHUNK, CHUNK), lanes] = scaled.astype(bf16)
 
     add_prefix(member, 0)
-    last = member
+    norm(member, 0)
+    last = None
     for place, step in enumerate(order):
         arrival(*second, step).wait_recv()
         add_prefix(partner(step), place + 1)
-        norm(last, place)
+        if last is not None:
+            norm(last, place)
         last = partner(step)
     norm(last, len(order))
 

time: 25.3 us -> 25.3 us (level)
  no operation moved by 1% of the time
where the time goes in v7:
time: 25.3 us; the launch traced here: 24.8 us
  Pallas kernels  23.5 us (93%)
  local copies, waits for them, and re-layouts  1.32 us (5%)
    pallas_call x1, Pallas kernels, body(): pl.pallas_call(functools.partial(kernel, n, heads, tokens), out_shape=jax...  23.5 us
    unnamed x1, local copies, waits for them, and re-layouts  1.32 us

profile of v7, /device:TPU:230, one launch (start us, length us, event | category | flops | bytes accessed | tf_op | source)
XLA Modules:
  0.0 24.8 jit_solution(17961875506954634010)
XLA Ops:
  0.0 23.5 %linear_attention.1 = bf16[1024,1024]{1,0:T(8,128)(2,1)S(1)} custom-call(bf16[1024,1024]{1,0:T(8,128)(2,1)} %q_hbm.1, bf16[1024,1024]{1,0:T(8,128)(2,1)} %k_hbm.1, bf16[1024,1024]{1,0:T(8,128)(2,1)} %v_hbm.1, f32[3,4,1024]{2,1,0:T(4,128)} %w_hbm.1, f32[1,1024]{1,0:T(1,128)} %bitcast.1), custom_call_target="tpu_custom_call" | custom-call | tf_op jit(solution)/shard_map/linear_attention/pallas_call | solution.py:321
  23.5 1.3 %copy.7 = bf16[1024,1024]{1,0:T(8,128)(2,1)} copy(bf16[1024,1024]{1,0:T(8,128)(2,1)S(1)} %linear_attention.1) | data formatting | bytes 4194304
